TPU v7x, 512 devices: a whole 4x4x16 slice. The times are simulated.
512 devices in a mesh: ta: 8 (over y, z_hi), ha: 4 (over x), wa: 16 (over z_lo, core).
Axes of the slice: x: 4, y: 4, z: 16 (z_hi: 2, z_lo: 8; z = z_hi * 8 + z_lo), core: 2. Of those that a mesh axis runs over, the one named last changes fastest.
Arguments:
- features: bfloat16 [16, 64, 256, 256], P('ta', 'ha', 'wa'), may hold values from -6 to 6
- conv_weight: bfloat16 [6912, 256], P('wa'), may hold values from -0.078125 to 0.078125
- down_weight: bfloat16 [2, 2, 256, 256], replicated, may hold values from -0.1875 to 0.1875
- grad_out: bfloat16 [16, 32, 128, 256], P('ta', 'ha', 'wa'), may hold values from -6 to 6
- crop_grad: bfloat16 [32768, 8, 8, 256], P(('ta', 'ha', 'wa')), may hold values from -6 to 6
- crop_owner: int32 [32768, 1], P(('ta', 'ha', 'wa')), may hold values from 0 to 63; in each aligned block of 64 rows (0 to 63, 64 to 127, ...) at most 2 rows name the same one
- crop_frame: int32 [32768], P(('ta', 'ha', 'wa')), may hold values from 0 to 1
- crop_row: int32 [32768], P(('ta', 'ha', 'wa')), may hold values from 0 to 8
- crop_col: int32 [32768], P(('ta', 'ha', 'wa')), may hold values from 0 to 8
- crop_valid: int32 [32768], P(('ta', 'ha', 'wa')), may hold values 0 or 1
Outputs:
- reduced: bfloat16 [16, 32, 128, 256], P('ta', 'ha', 'wa')
- grad_in: bfloat16 [16, 64, 256, 256], P('ta', 'ha', 'wa')
Inputs may be any that keep to these rules, and one draw needn't show every extreme that they name: `crop_owner`: among one device's 64 crops at most 2 name the same owner, a bound that some block reaches; the owner is the tile of the same time slab whose height index is the value divided by the number of width tiles and whose width index is the remainder. `crop_frame`: frame of the crop within the time slab of the device that holds it. `crop_valid`: padding crops carry gradients that are ignored.
All inputs are finite; a program needn't handle non-finite values. No bound on the sum of `crop_valid` on one device may be relied on, other than what follows from the above.
Results may differ from a plain program's by a relative error of at most 0.0049.
Values may be sent and summed in bfloat16 or wider, within the bound.
A program may use at most 64 MiB of HBM per device.

v0:
```python
import jax
import jax.numpy as jnp
from jax import lax
from jax.sharding import PartitionSpec as P

CH = 8
CW = 8
CAP = 2


def extended(block, sides, width):
    for axis, dim in sides:
        count = lax.axis_size(axis)
        forward = [(i, i + 1) for i in range(count - 1)]
        backward = [(target, source) for source, target in forward]
        low = lax.ppermute(
            lax.slice_in_dim(block, block.shape[dim] - width, None, axis=dim), axis, forward
        )
        high = lax.ppermute(lax.slice_in_dim(block, 0, width, axis=dim), axis, backward)
        block = jnp.concatenate([low, block, high], axis=dim)
    return block


def from_behind(value, axis, steps):
    count = lax.axis_size(axis)
    first, last = (max(0, -steps), min(count, count - steps))
    return lax.ppermute(value, axis, [(source, source + steps) for source in range(first, last)])


def convolve(padded, kernel_taps, frames, rows, cols):
    width = kernel_taps.shape[-1]
    summed = jnp.zeros((frames * rows * cols, width), jnp.float32)
    for frame_off in range(3):
        windows = []
        for row_off in range(3):
            for col_off in range(3):
                windows.append(
                    padded[
                        frame_off : frame_off + frames,
                        row_off : row_off + rows,
                        col_off : col_off + cols,
                        :,
                    ]
                )
        stacked = jnp.concatenate(windows, -1).reshape(frames * rows * cols, 9 * width)
        tap_block = kernel_taps[frame_off * 9 : (frame_off + 1) * 9].reshape(9 * width, width)
        summed = summed + jnp.dot(stacked, tap_block, preferred_element_type=jnp.float32)
    return summed.reshape(frames, rows, cols, width)


def widen(block):
    return extended(block, (("ha", 1), ("wa", 2)), 1)


def per_device(
    features,
    conv_weight,
    down_weight,
    grad_out,
    crop_grad,
    crop_owner,
    crop_frame,
    crop_row,
    crop_col,
    crop_valid,
):
    frames, rows, cols, width = features.shape
    height_tiles = lax.axis_size("ha")
    width_tiles = lax.axis_size("wa")
    owners_all = height_tiles * width_tiles
    slots_all = owners_all * CAP
    count = crop_owner.shape[0]
    owner_id = crop_owner[:, 0]
    onehot = (owner_id[:, None] == jnp.arange(owners_all, dtype=jnp.int32)[None, :]).astype(
        jnp.int32
    )
    earlier = jnp.cumsum(onehot, 0) - onehot
    slot_rank = jnp.sum(earlier * onehot, 1)
    target = owner_id * CAP + slot_rank
    placing = target[:, None] == jnp.arange(slots_all, dtype=jnp.int32)[None, :]
    weighted = crop_grad * crop_valid.astype(jnp.bfloat16)[:, None, None, None]
    packed = jnp.dot(
        placing.astype(jnp.bfloat16).T,
        weighted.reshape(count, -1),
        preferred_element_type=jnp.float32,
    ).astype(jnp.bfloat16)
    place_meta = jnp.stack([crop_frame, crop_row, crop_col], 1)
    meta_sent = jnp.sum(placing.astype(jnp.int32)[:, :, None] * place_meta[:, None, :], 0)
    received, got_meta = (
        lax.all_to_all(packed, ("ha", "wa"), split_axis=0, concat_axis=0, tiled=True),
        lax.all_to_all(meta_sent, ("ha", "wa"), split_axis=0, concat_axis=0, tiled=True),
    )
    row_steps = jnp.arange(CH, dtype=jnp.int32)
    col_steps = jnp.arange(CW, dtype=jnp.int32)
    cell_index = (
        (got_meta[:, 0, None, None] * rows + got_meta[:, 1, None, None] + row_steps[None, :, None])
        * cols
        + got_meta[:, 2, None, None]
        + col_steps[None, None, :]
    )
    crop_terms = (
        jnp.zeros((frames * rows * cols, width), jnp.float32)
        .at[cell_index.reshape(-1)]
        .add(received.reshape(-1, width).astype(jnp.float32))
    )
    gathered = lax.all_gather(conv_weight, "wa", axis=0, tiled=True)
    kernel_taps = gathered.reshape(27, width, width)
    past = from_behind(features, "ta", 1)
    padded = widen(jnp.concatenate([past, features], 0))
    preact = convolve(padded, kernel_taps, frames, rows, cols)
    sigmoid_h = jax.nn.sigmoid(preact)
    section_out = (features.astype(jnp.float32) + preact * sigmoid_h).astype(jnp.bfloat16)
    down_mat = down_weight.reshape(4 * width, width)
    pooled = (
        section_out.reshape(frames, rows // 2, 2, cols // 2, 2, width)
        .transpose(0, 1, 3, 2, 4, 5)
        .reshape(-1, 4 * width)
    )
    reduced = (
        jnp.dot(pooled, down_mat, preferred_element_type=jnp.float32)
        .astype(jnp.bfloat16)
        .reshape(frames, rows // 2, cols // 2, width)
    )
    spread = jnp.dot(grad_out.reshape(-1, width), down_mat.T, preferred_element_type=jnp.float32)
    spread = (
        spread.reshape(frames, rows // 2, cols // 2, 2, 2, width)
        .transpose(0, 1, 3, 2, 4, 5)
        .reshape(frames, rows, cols, width)
    )
    grad_pre = (spread * sigmoid_h * (1.0 + preact * (1.0 - sigmoid_h))).astype(jnp.bfloat16)
    flipped = jnp.transpose(kernel_taps[::-1], (0, 2, 1))
    future = from_behind(grad_pre, "ta", -1)
    back_pad = widen(jnp.concatenate([grad_pre, future], 0))
    through = convolve(back_pad, flipped, frames, rows, cols)
    grad_in = (spread + through + crop_terms.reshape(frames, rows, cols, width)).astype(
        jnp.bfloat16
    )
    return (reduced, grad_in)


def solution(mesh):
    in_specs = (
        P("ta", "ha", "wa", None),
        P("wa", None),
        P(),
        P("ta", "ha", "wa", None),
        P(("ta", "ha", "wa"), None, None, None),
        P(("ta", "ha", "wa"), None),
        P(("ta", "ha", "wa")),
        P(("ta", "ha", "wa")),
        P(("ta", "ha", "wa")),
        P(("ta", "ha", "wa")),
    )
    out_specs = (P("ta", "ha", "wa", None), P("ta", "ha", "wa", None))
    return jax.shard_map(
        per_device, mesh=mesh, in_specs=in_specs, out_specs=out_specs, check_vma=False
    )
```

profile of v0, /device:TPU:29, one launch (start us, length us, event | category | flops | bytes accessed | tf_op | source)
XLA Modules:
  0.0 448.0 jit_solution(8883349491360563896)
XLA Ops:
  7.2 0.8 fusion.23
  8.1 0.8 select_reduce_fusion
  8.9 0.7 fusion.25
  9.6 0.7 pad_add_fusion
  10.4 0.8 copy.87
  11.2 16.5 %all-to-all-start = ((s32[64,2,3]{2,1,0:T(2,128)}), s32[64,2,3]{2,1,0:T(2,128)S(1)}, u32[]{:S(2)}, u32[]{:S(2)}) async-start(s32[64,2,3]{2,1,0:T(2,128)} %bitcast.28), calls=%async_computation | async-start | bytes 131072 | tf_op jit(solution)/shard_map/all_to_all | solution.py:91
  27.7 0.7 convert_element_type.44
  28.3 1.8 broadcast_multiply_fusion
  30.1 1.3 copy.92
  31.4 3.3 convolution_convert_fusion
  34.8 7.7 %all_to_all.17 = bf16[64,2,16384]{2,1,0:T(2,128)(2,1)} reshape(bf16[128,16384]{1,0:T(8,128)(2,1)} %convolution_convert_fusion) | data formatting | bytes 8388608 | tf_op jit(solution)/shard_map/all_to_all | solution.py:90
  42.4 13.4 %all-to-all-start.1 = ((bf16[64,2,16384]{2,1,0:T(2,128)(2,1)}), bf16[64,2,16384]{2,1,0:T(2,128)(2,1)}, u32[]{:S(2)}, u32[]{:S(2)}) async-start(bf16[64,2,16384]{2,1,0:T(2,128)(2,1)} %all_to_all.17), calls=%async_computation.1 | async-start | bytes 8388608 | tf_op jit(solution)/shard_map/all_to_all | solution.py:90
  55.9 0.7 all-gather.2.cloned.1.call-update
  56.6 7.9 %collective-permute-start = (bf16[2,16,16,256]{3,2,1,0:T(8,128)(2,1)S(1)}, bf16[2,16,16,256]{3,2,1,0:T(8,128)(2,1)S(1)}, u32[]{:S(2)}, u32[]{:S(2)}) collective-permute-start(bf16[2,16,16,256]{3,2,1,0:T(8,128)(2,1)S(1)} %copy-done.3), channel_id=1, source_target_pairs={{0,64},{64,128},{128,192},{192,256},{256,320},{320,384},{384,448},... | collective-permute-start | bytes 786440 | tf_op jit(solution)/shard_map/ppermute | solution.py:27
  64.5 0.3 convolution_bitcast_fusion
  64.9 0.4 copy.74
  65.7 109.0 %collective-permute-done = bf16[2,16,16,256]{3,2,1,0:T(8,128)(2,1)S(1)} collective-permute-done((bf16[2,16,16,256]{3,2,1,0:T(8,128)(2,1)S(1)}, bf16[2,16,16,256]{3,2,1,0:T(8,128)(2,1)S(1)}, u32[]{:S(2)}, u32[]{:S(2)}) %collective-permute-start) | collective-permute-done | bytes 262176 | tf_op jit(solution)/shard_map/ppermute | solution.py:27
  174.8 2.9 collective-permute-start.1
  177.7 2.4 collective-permute-start.2
  180.3 0.3 add.134
  180.6 2.3 collective-permute-done.2
  183.0 1.9 collective-permute-start.3
  184.9 3.1 collective-permute-start.4
  188.1 4.6 %collective-permute-done.4 = bf16[4,18,1,256]{3,2,1,0:T(2,128)(2,1)S(1)} collective-permute-done((bf16[4,18,1,256]{3,2,1,0:T(2,128)(2,1)S(1)}, bf16[4,18,1,256]{3,2,1,0:T(2,128)(2,1)S(1)}, u32[]{:S(2)}, u32[]{:S(2)}) %collective-permute-start.4) | collective-permute-done | bytes 36896 | tf_op jit(solution)/shard_map/ppermute | solution.py:19
  192.7 0.6 pad_maximum_fusion
  193.3 1.0 slice_dynamic-update-slice_fusion.29
  194.3 1.0 fusion.18
  195.3 1.1 slice_dynamic-update-slice_fusion.28
  196.5 1.1 slice_dynamic-update-slice_fusion.27
  197.5 0.8 constant_dynamic-update-slice_fusion.3
  198.3 0.9 slice_dynamic-update-slice_fusion.33
  199.3 1.1 slice_dynamic-update-slice_fusion.26
  200.4 1.0 slice_dynamic-update-slice_fusion.25
  201.4 1.0 fusion.17
  202.4 1.2 slice_dynamic-update-slice_fusion.24
  203.6 42.9 %all-gather.2.cloned.1.call-done = bf16[6912,256]{1,0:T(8,128)(2,1)} async-done(((bf16[432,256]{1,0:T(8,128)(2,1)}), bf16[6912,256]{1,0:T(8,128)(2,1)}) %all-gather.2.cloned.1.call-update) | async-done | bytes 3538960 | tf_op jit(solution)/shard_map/all_gather | solution.py:106
  246.5 2.9 fusion.2
  249.6 2.4 convolution_add_fusion.3
  252.0 2.4 convolution_add_fusion.2
  254.5 0.3 fusion.7
  254.7 13.9 %collective-permute-start.5 = (bf16[2,16,16,256]{3,2,1,0:T(8,128)(2,1)S(1)}, bf16[2,16,16,256]{3,2,1,0:T(8,128)(2,1)S(1)}, u32[]{:S(2)}, u32[]{:S(2)}) collective-permute-start(bf16[2,16,16,256]{3,2,1,0:T(8,128)(2,1)S(1)} %get-tuple-element.75), channel_id=1, source_target_pairs={{64,0},{128,64},{192,128},{256,192},{320,256},{384,320},{448,384},... | collective-permute-start | bytes 786440 | tf_op jit(solution)/shard_map/ppermute | solution.py:27
  269.2 2.4 reverse_bitcast_fusion
  271.6 1.7 fusion.26
  273.3 1.3 collective-permute-done.5
  274.6 2.7 collective-permute-start.6
  277.2 2.6 collective-permute-start.7
  279.8 0.9 convolution_convert_fusion.1
  280.7 2.4 copy.76
  283.1 1.5 copy.77
  284.6 1.6 copy.78
  286.4 89.7 %collective-permute-start.8 = (bf16[4,18,1,256]{3,2,1,0:T(2,128)(2,1)S(1)}, bf16[4,18,1,256]{3,2,1,0:T(2,128)(2,1)S(1)}, u32[]{:S(2)}, u32[]{:S(2)}) collective-permute-start(bf16[4,18,1,256]{3,2,1,0:T(2,128)(2,1)S(1)} %get-tuple-element.54), channel_id=1, source_target_pairs={{0,1},{1,2},{2,3},{3,4},{4,5},{5,6},{6,7},{7,8},{8,9},{9,10},{10,1... | collective-permute-start | bytes 110600 | tf_op jit(solution)/shard_map/ppermute | solution.py:16
  376.0 1.9 collective-permute-start.9
  378.1 3.6 collective-permute-done.9
  381.7 0.6 pad_maximum_fusion.1
  382.4 0.2 slice_dynamic-update-slice_fusion.5
  383.1 0.2 slice_dynamic-update-slice_fusion
  383.3 0.9 copy-done.4
  384.2 0.8 fusion.29
  385.0 0.8 convolution_add_fusion.1
  385.8 0.8 convolution_add_fusion
  386.6 8.2 %reshape.228 = f32[8192,256]{1,0:T(8,128)} reshape(bf16[64,2,16384]{2,1,0:T(2,128)(2,1)} %all-to-all-done.1) | data formatting | bytes 12582912 | tf_op jit(solution)/shard_map/convert_element_type | solution.py:104
  394.8 44.7 %scatter_custom_fusion = f32[512,256]{1,0:T(8,128)S(1)} fusion(s32[8192]{0:T(1024)S(1)} %bitcast.83, f32[8192,256]{1,0:T(8,128)} %reshape.228, f32[]{:T(128)} %constant.7.clone.1), kind=kCustom, calls=%fused_computation.96 | custom fusion | flops 2097152 | bytes 524800 | tf_op jit(solution)/shard_map/scatter-add | solution.py:104
  439.5 0.9 fusion.5
  440.4 0.7 copy.84
  (48 shorter events, 2.6 us)
Async XLA Ops:
  7.2 57.4 %copy-start = (bf16[2,2,256,256]{3,2,1,0:T(8,128)(2,1)S(1)}, bf16[2,2,256,256]{3,2,1,0:T(8,128)(2,1)}, u32[]{:S(2)}) copy-start(bf16[2,2,256,256]{3,2,1,0:T(8,128)(2,1)} %param.12) | copy-start | bytes 1572868
  11.2 31.2 %all-to-all-start = ((s32[64,2,3]{2,1,0:T(2,128)}), s32[64,2,3]{2,1,0:T(2,128)S(1)}, u32[]{:S(2)}, u32[]{:S(2)}) async-start(s32[64,2,3]{2,1,0:T(2,128)} %bitcast.28), calls=%async_computation | async-start | bytes 131072 | tf_op jit(solution)/shard_map/all_to_all | solution.py:91
  42.4 14.1 %copy-start.3 = (bf16[2,16,16,256]{3,2,1,0:T(8,128)(2,1)S(1)}, bf16[2,16,16,256]{3,2,1,0:T(8,128)(2,1)}, u32[]{:S(2)}) copy-start(bf16[2,16,16,256]{3,2,1,0:T(8,128)(2,1)} %param.10) | copy-start | bytes 786436
  42.4 22.1 %copy-start.5 = (bf16[2,8,8,256]{3,2,1,0:T(8,128)(2,1)S(1)}, bf16[2,8,8,256]{3,2,1,0:T(8,128)(2,1)}, u32[]{:S(2)}) copy-start(bf16[2,8,8,256]{3,2,1,0:T(8,128)(2,1)} %param.13) | copy-start | bytes 196612
  42.4 344.2 %all-to-all-start.1 = ((bf16[64,2,16384]{2,1,0:T(2,128)(2,1)}), bf16[64,2,16384]{2,1,0:T(2,128)(2,1)}, u32[]{:S(2)}, u32[]{:S(2)}) async-start(bf16[64,2,16384]{2,1,0:T(2,128)(2,1)} %all_to_all.17), calls=%async_computation.1 | async-start | bytes 8388608 | tf_op jit(solution)/shard_map/all_to_all | solution.py:90
  55.8 190.7 %all-gather.2.cloned.1.call-start = ((), (), s32[]{:S(2)}) async-start(), calls=%async_computation.2 | async-start | bytes 3760128 | tf_op jit(solution)/shard_map/all_gather | solution.py:106
  56.6 118.1 %collective-permute-start = (bf16[2,16,16,256]{3,2,1,0:T(8,128)(2,1)S(1)}, bf16[2,16,16,256]{3,2,1,0:T(8,128)(2,1)S(1)}, u32[]{:S(2)}, u32[]{:S(2)}) collective-permute-start(bf16[2,16,16,256]{3,2,1,0:T(8,128)(2,1)S(1)} %copy-done.3), channel_id=1, source_target_pairs={{0,64},{64,128},{128,192},{192,256},{256,320},{320,384},{384,448},... | collective-permute-start | bytes 786440 | tf_op jit(solution)/shard_map/ppermute | solution.py:27
  174.8 5.8 %collective-permute-start.1 = (bf16[4,1,16,256]{3,2,1,0:T(8,128)(2,1)S(1)}, bf16[4,1,16,256]{3,2,1,0:T(8,128)(2,1)S(1)}, u32[]{:S(2)}, u32[]{:S(2)}) collective-permute-start(bf16[4,1,16,256]{3,2,1,0:T(8,128)(2,1)S(1)} %get-tuple-element.77), channel_id=1, source_target_pairs={{0,16},{16,32},{32,48},{1,17},{17,33},{33,49},{2,18},{18,34},{34,5... | collective-permute-start | bytes 98312 | tf_op jit(solution)/shard_map/ppermute | solution.py:16
  177.7 5.2 %collective-permute-start.2 = (bf16[4,1,16,256]{3,2,1,0:T(8,128)(2,1)S(1)}, bf16[4,1,16,256]{3,2,1,0:T(8,128)(2,1)S(1)}, u32[]{:S(2)}, u32[]{:S(2)}) collective-permute-start(bf16[4,1,16,256]{3,2,1,0:T(8,128)(2,1)S(1)} %get-tuple-element.78), channel_id=1, source_target_pairs={{16,0},{32,16},{48,32},{17,1},{33,17},{49,33},{18,2},{34,18},{50,3... | collective-permute-start | bytes 98312 | tf_op jit(solution)/shard_map/ppermute | solution.py:19
  183.0 5.1 %collective-permute-start.3 = (bf16[4,18,1,256]{3,2,1,0:T(2,128)(2,1)S(1)}, bf16[4,18,1,256]{3,2,1,0:T(2,128)(2,1)S(1)}, u32[]{:S(2)}, u32[]{:S(2)}) collective-permute-start(bf16[4,18,1,256]{3,2,1,0:T(2,128)(2,1)S(1)} %get-tuple-element.58), channel_id=1, source_target_pairs={{0,1},{1,2},{2,3},{3,4},{4,5},{5,6},{6,7},{7,8},{8,9},{9,10},{10,1... | collective-permute-start | bytes 110600 | tf_op jit(solution)/shard_map/ppermute | solution.py:16
  184.9 7.8 %collective-permute-start.4 = (bf16[4,18,1,256]{3,2,1,0:T(2,128)(2,1)S(1)}, bf16[4,18,1,256]{3,2,1,0:T(2,128)(2,1)S(1)}, u32[]{:S(2)}, u32[]{:S(2)}) collective-permute-start(bf16[4,18,1,256]{3,2,1,0:T(2,128)(2,1)S(1)} %get-tuple-element.57), channel_id=1, source_target_pairs={{1,0},{2,1},{3,2},{4,3},{5,4},{6,5},{7,6},{8,7},{9,8},{10,9},{11,1... | collective-permute-start | bytes 110600 | tf_op jit(solution)/shard_map/ppermute | solution.py:19
  246.5 3.1 copy-start.2
  254.7 19.8 %collective-permute-start.5 = (bf16[2,16,16,256]{3,2,1,0:T(8,128)(2,1)S(1)}, bf16[2,16,16,256]{3,2,1,0:T(8,128)(2,1)S(1)}, u32[]{:S(2)}, u32[]{:S(2)}) collective-permute-start(bf16[2,16,16,256]{3,2,1,0:T(8,128)(2,1)S(1)} %get-tuple-element.75), channel_id=1, source_target_pairs={{64,0},{128,64},{192,128},{256,192},{320,256},{384,320},{448,384},... | collective-permute-start | bytes 786440 | tf_op jit(solution)/shard_map/ppermute | solution.py:27
  274.6 11.7 %collective-permute-start.6 = (bf16[4,1,16,256]{3,2,1,0:T(8,128)(2,1)S(1)}, bf16[4,1,16,256]{3,2,1,0:T(8,128)(2,1)S(1)}, u32[]{:S(2)}, u32[]{:S(2)}) collective-permute-start(bf16[4,1,16,256]{3,2,1,0:T(8,128)(2,1)S(1)} %get-tuple-element.73), channel_id=1, source_target_pairs={{0,16},{16,32},{32,48},{1,17},{17,33},{33,49},{2,18},{18,34},{34,5... | collective-permute-start | bytes 98312 | tf_op jit(solution)/shard_map/ppermute | solution.py:16
  277.2 9.0 %collective-permute-start.7 = (bf16[4,1,16,256]{3,2,1,0:T(8,128)(2,1)S(1)}, bf16[4,1,16,256]{3,2,1,0:T(8,128)(2,1)S(1)}, u32[]{:S(2)}, u32[]{:S(2)}) collective-permute-start(bf16[4,1,16,256]{3,2,1,0:T(8,128)(2,1)S(1)} %get-tuple-element.74), channel_id=1, source_target_pairs={{16,0},{32,16},{48,32},{17,1},{33,17},{49,33},{18,2},{34,18},{50,3... | collective-permute-start | bytes 98312 | tf_op jit(solution)/shard_map/ppermute | solution.py:19
  286.4 91.7 %collective-permute-start.8 = (bf16[4,18,1,256]{3,2,1,0:T(2,128)(2,1)S(1)}, bf16[4,18,1,256]{3,2,1,0:T(2,128)(2,1)S(1)}, u32[]{:S(2)}, u32[]{:S(2)}) collective-permute-start(bf16[4,18,1,256]{3,2,1,0:T(2,128)(2,1)S(1)} %get-tuple-element.54), channel_id=1, source_target_pairs={{0,1},{1,2},{2,3},{3,4},{4,5},{5,6},{6,7},{7,8},{8,9},{9,10},{10,1... | collective-permute-start | bytes 110600 | tf_op jit(solution)/shard_map/ppermute | solution.py:16
  376.0 5.7 %collective-permute-start.9 = (bf16[4,18,1,256]{3,2,1,0:T(2,128)(2,1)S(1)}, bf16[4,18,1,256]{3,2,1,0:T(2,128)(2,1)S(1)}, u32[]{:S(2)}, u32[]{:S(2)}) collective-permute-start(bf16[4,18,1,256]{3,2,1,0:T(2,128)(2,1)S(1)} %get-tuple-element.53), channel_id=1, source_target_pairs={{1,0},{2,1},{3,2},{4,3},{5,4},{6,5},{7,6},{8,7},{9,8},{10,9},{11,1... | collective-permute-start | bytes 110600 | tf_op jit(solution)/shard_map/ppermute | solution.py:19
  383.0 1.3 copy-start.4
  383.3 1.7 copy-start.1
Sparse Core Ops, SparseCore 0:
  58.7 187.7 all-gather.1
where the time goes:
time: 449 us; the launch traced here: 448 us
  waiting for transfers between devices  164 us (37%)
  starting transfers between devices  159 us (35%)
  other arithmetic  55.3 us (12%)
  local copies, waits for them, and re-layouts  40.2 us (9%)
  matrix products  14.6 us (3%)
  between operations  14.5 us (3%)
    ppermute x2, waiting for transfers between devices, from_behind(): lax.ppermute(value, axis, [(source, source + steps) for source in range(f...  110 us
    ppermute x4, starting transfers between devices, extended(): lax.ppermute(lax.slice_in_dim(block, block.shape[dim] - width, None, axis...  97.2 us
    scatter-add x1, other arithmetic, per_device(): crop_terms = jnp.zeros((frames * rows * cols, width), jnp.float32).at[cel...  44.7 us
    all_gather x1, waiting for transfers between devices, per_device(): gathered = lax.all_gather(conv_weight, 'wa', axis=0, tiled=True)  42.9 us
    ppermute x2, starting transfers between devices, from_behind(): lax.ppermute(value, axis, [(source, source + steps) for source in range(f...  21.9 us
    all_to_all x1, starting transfers between devices, per_device(): lax.all_to_all(meta_sent, ('ha', 'wa'), split_axis=0, concat_axis=0, tile...  16.5 us
    all_to_all x1, starting transfers between devices, per_device(): lax.all_to_all(packed, ('ha', 'wa'), split_axis=0, concat_axis=0, tiled=T...  13.4 us
    unnamed x32, local copies, waits for them, and re-layouts  11.2 us
  transfers between devices with their start and end apart: 13, of which 6 were waited for; matrix products, arithmetic and copies ran while one was open for 10% of the time, Pallas kernels for 0%

commit v1 on v0

v1 whole, which is shorter than its diff:
```python
import functools

import jax
import jax.numpy as jnp
from jax import lax
from jax.experimental import pallas as pl
from jax.experimental.pallas import tpu as pltpu
from jax.sharding import PartitionSpec as P

MESH = pl.DeviceIdType.MESH
CAP = 2


def place():
    slab, x, strip = lax.axis_index("ta"), lax.axis_index("ha"), lax.axis_index("wa")
    return slab // 2, (slab % 2) * 8 + strip // 2, x, strip % 2


def at(y, z, x, core):
    y, z, x = (y + 4) % 4, (z + 16) % 16, (x + 4) % 4
    return (y * 2 + z // 8, x, (z % 8) * 2 + core)


class Copies:
    def __init__(self, send_sems, recv_sems):
        self.send_sems, self.recv_sems, self.used, self.sent = send_sems, recv_sems, 0, []

    def make(self, src, dst, device):
        slot = self.used
        self.used += 1
        return pltpu.make_async_remote_copy(
            src_ref=src,
            dst_ref=dst,
            send_sem=self.send_sems.at[slot],
            recv_sem=self.recv_sems.at[slot],
            device_id=device,
            device_id_type=MESH,
        )

    def start(self, src, dst, device):
        copy = self.make(src, dst, device)
        copy.start()
        self.sent.append(copy)
        return copy


def greet(devices):
    barrier = pltpu.get_barrier_semaphore()
    for device in devices:
        pl.semaphore_signal(barrier, inc=1, device_id=device, device_id_type=MESH)
    pl.semaphore_wait(barrier, len(devices))


def edge_columns(ext, edge, frame):
    rows, cols, width = ext.shape[1:]
    flat = ext[frame].reshape(rows * cols, width)
    row = lax.broadcasted_iota(jnp.int32, (edge.shape[2], rows * cols), 0)
    cell = lax.broadcasted_iota(jnp.int32, (edge.shape[2], rows * cols), 1)
    for side, col in ((0, 0), (1, cols - 1)):
        pick = jnp.where(cell == row * cols + col, 1.0, 0.0).astype(jnp.bfloat16)
        edge[side, frame] = jnp.dot(pick, flat, preferred_element_type=jnp.float32).astype(
            jnp.bfloat16
        )


class Halo:
    def __init__(self, copies, tile, ext, left, right, relay, edge, own, other, step):
        self.copies, self.tile, self.ext, self.left, self.right = copies, tile, ext, left, right
        self.relay, self.edge, self.own, self.other, self.step = relay, edge, own, other, step

    def first(self):
        y, z, x, core = place()
        self.up = self.copies.start(self.tile.at[0], self.relay.at[0], at(y, z + 4, x, core))
        self.down = self.copies.start(self.tile.at[1], self.relay.at[1], at(y, z - 4, x, core))

    def own_rows(self):
        y, z, x, core = place()
        ext, own = self.ext, self.own
        rows = self.tile.shape[1]
        self.rows_own = [
            self.copies.start(
                self.tile.at[:, pl.ds(rows - 1, 1)],
                ext.at[pl.ds(own, 2), pl.ds(0, 1)],
                at(y, z, x + 1, core),
            ),
            self.copies.start(
                self.tile.at[:, pl.ds(0, 1)],
                ext.at[pl.ds(own, 2), pl.ds(rows + 1, 1)],
                at(y, z, x - 1, core),
            ),
        ]
        ext[own : own + 2, 1 : rows + 1] = self.tile[...]

    def forward(self):
        y, z, x, core = place()
        rows = self.tile.shape[1]
        self.far = []
        for frame, copy, turn in ((0, self.up, 4), (1, self.down, -4)):
            source_hi = ((z - turn + 16) % 16) // 8
            y_to = y + source_hi if self.step == 1 else y - 1 + source_hi
            copy.wait_recv()
            self.far.append(
                self.copies.start(
                    self.relay.at[frame],
                    self.ext.at[self.other + frame, pl.ds(1, rows)],
                    at(y_to, z + turn, x, core),
                )
            )

    def finish(self):
        y, z, x, core = place()
        ext, other = self.ext, self.other
        rows = self.tile.shape[1]
        for copy in self.rows_own:
            copy.wait_recv()
        for frame in range(2):
            edge_columns(ext, self.edge, self.own + frame)
        for copy in self.far:
            copy.wait_recv()
        borders = [
            self.copies.start(
                ext.at[pl.ds(other, 2), pl.ds(rows, 1)],
                ext.at[pl.ds(other, 2), pl.ds(0, 1)],
                at(y, z, x + 1, core),
            ),
            self.copies.start(
                ext.at[pl.ds(other, 2), pl.ds(1, 1)],
                ext.at[pl.ds(other, 2), pl.ds(rows + 1, 1)],
                at(y, z, x - 1, core),
            ),
        ]
        for copy in borders:
            copy.wait_recv()
        for frame in range(2):
            edge_columns(ext, self.edge, other + frame)
        sides = [
            self.copies.start(self.edge.at[1], self.left, at(y, z + core, x, 1 - core)),
            self.copies.start(self.edge.at[0], self.right, at(y, z - 1 + core, x, 1 - core)),
        ]
        for copy in sides:
            copy.wait_recv()


def halo_partners():
    y, z, x, core = place()
    return [
        at(y, z + 4, x, core),
        at(y, z - 4, x, core),
        at(y + 1, z + 4, x, core),
        at(y - 1, z - 4, x, core),
        at(y + 1, z - 4, x, core),
        at(y - 1, z + 4, x, core),
        at(y, z, x + 1, core),
        at(y, z, x - 1, core),
        at(y, z, x, 1 - core),
        at(y, z + 1, x, core),
        at(y, z - 1, x, core),
        at(y, z - 1 + 2 * core, x, 1 - core),
    ]


def gather_kernel(
    tile, shard, packed, cells, ext, left, right, taps, crops, places,
    relay, edge, cross, keep, send_sems, recv_sems, local_sems,
):
    y, z, x, core = place()
    strip = z % 8
    copies = Copies(send_sems, recv_sems)
    greet(
        halo_partners()
        + [
            at(y, z, x + 1, 1 - core),
            at(y, z, x - 1, 1 - core),
            at(y, z, x + 2, core),
            at(y, z, x + 2, 1 - core),
            at(y + 1, z, x, core),
            at(y - 1, z, x, core),
        ]
    )
    halo = Halo(copies, tile, ext, left, right, relay, edge, 2, 0, 1)
    half = pl.ds(pl.multiple_of((y % 2) * 128, 128), 128)
    mine = x * 2 + core
    turn = 1 - 2 * core

    def lane(offset):
        return ((strip + offset + 8) % 8) * 2 + core

    across = (x + 2) % 4
    cross_in = [
        copies.start(
            packed.at[across * 2 + (core + flip) % 2],
            cross.at[flip],
            at(y, z, x + turn, core),
        )
        for flip in range(2)
    ]
    halo.first()
    ring = {}
    for way in (1, -1):
        ring[way] = copies.start(
            shard.at[:, half], taps.at[lane(0), :, half], at(y, z + way, x, core)
        )
    halo.own_rows()
    got = []
    for away in (1, -1):
        for flip in range(2):
            to = (core + flip) % 2
            got.append(
                copies.start(
                    packed.at[((x + away + 4) % 4) * 2 + to],
                    crops.at[:, mine],
                    at(y, z, x + away, to),
                )
            )
    got.append(
        copies.start(packed.at[x * 2 + 1 - core], crops.at[:, mine], at(y, z, x, 1 - core))
    )
    for away in (1, 2, 3):
        for flip in range(2):
            to = (core + flip) % 2
            got.append(
                copies.start(
                    cells.at[((x + away) % 4) * 2 + to], places.at[mine], at(y, z, x + away, to)
                )
            )
    got.append(
        copies.start(cells.at[x * 2 + 1 - core], places.at[mine], at(y, z, x, 1 - core))
    )
    got.append(copies.start(shard, taps.at[lane(0)], at(y, z, x, 1 - core)))
    own_shard = pltpu.make_async_copy(shard, taps.at[lane(0)], local_sems.at[0])
    own_shard.start()
    own_in = pltpu.make_async_copy(packed.at[mine], keep, local_sems.at[1])
    own_in.start()
    places[mine] = cells[mine]

    swaps = {}

    def swap(offset, y_to):
        piece = taps.at[lane(offset), :, half]
        swaps[offset] = copies.start(piece, piece, at(y_to, z, x, core))

    def ring_step(step):
        for way in (1, -1):
            ring[way].wait_recv()
            offset = -way * step
            if step < 3:
                piece = taps.at[lane(offset), :, half]
                ring[way] = copies.start(piece, piece, at(y, z + way, x, core))
            swap(offset, y + way)

    ring_step(1)
    ring_step(2)
    own_in.wait()
    own_out = pltpu.make_async_copy(keep, crops.at[:, mine], local_sems.at[2])
    own_out.start()

    def cross_out(flip):
        cross_in[flip].wait_recv()
        source = ((x - turn + 4) % 4) * 2 + core
        got.append(
            copies.start(
                cross.at[flip],
                crops.at[:, source],
                at(y, z, x + turn, (core + flip) % 2),
            )
        )

    ring_step(3)
    last = taps.at[lane(4), :, half]
    piece = taps.at[lane(-3 * turn), :, half]
    ring_last = copies.start(piece, piece, at(y, z + turn, x, core))
    cross_out(0)
    halo.forward()
    cross_out(1)
    ring_last.wait_recv()
    swaps[4] = copies.start(last, last, at(y + turn, z, x, core))
    for offset in (1, -1, 2, -2, 3, -3, 4):
        swaps[offset].wait_recv()
        whole = taps.at[lane(offset)]
        got.append(copies.start(whole, whole, at(y, z, x, 1 - core)))
    halo.finish()
    assert copies.used == 48, copies.used
    for copy in got:
        copy.wait_recv()
    own_shard.wait()
    own_out.wait()
    for copy in copies.sent:
        copy.wait_send()


def scatter_kernel(
    tile, part, ext, left, right, total,
    relay, edge, in_up, in_down, out_up, out_down,
    send_sems, recv_sems, up_send, up_recv, down_send, down_recv,
):
    y, z, x, core = place()
    strip = z % 8
    copies = Copies(send_sems, recv_sems)
    greet(halo_partners())
    halo = Halo(copies, tile, ext, left, right, relay, edge, 0, 2, -1)
    halo.first()
    halo.own_rows()

    def chain(goal, chunk, way):
        landing, leaving, sends, recvs = (
            (in_up, out_up, up_send, up_recv) if way == 1 else (in_down, out_down, down_send, down_recv)
        )
        return pltpu.make_async_remote_copy(
            src_ref=leaving.at[goal, chunk],
            dst_ref=landing.at[goal, chunk],
            send_sem=sends.at[goal, chunk],
            recv_sem=recvs.at[goal, chunk],
            device_id=at(y, z + way, x, core),
            device_id_type=MESH,
        )

    def advance(step, chunk, way):
        rank = strip if way == 1 else 7 - strip
        ahead = 7 - step + rank

        @pl.when(rank <= step)
        def _():
            goal = ahead if way == 1 else 7 - ahead
            copy = chain(goal, chunk, way)
            landing, leaving = (in_up, out_up) if way == 1 else (in_down, out_down)

            @pl.when(rank > 0)
            def _():
                copy.wait_recv()
                summed = part[goal, chunk].astype(jnp.float32) + landing[goal, chunk].astype(
                    jnp.float32
                )
                leaving[goal, chunk] = summed.astype(jnp.bfloat16)

            @pl.when(rank == 0)
            def _():
                leaving[goal, chunk] = part[goal, chunk]

            copy.start()

    for step in range(7):
        for chunk in range(2):
            for way in (1, -1):
                advance(step, chunk, way)
        if step == 3:
            halo.forward()
    halo.finish()
    for chunk in range(2):
        total[chunk] = part[strip, chunk].astype(jnp.float32)
        for way in (1, -1):
            landing = in_up if way == 1 else in_down

            @pl.when((strip if way == 1 else 7 - strip) > 0)
            def _():
                chain(strip, chunk, way).wait_recv()
                total[chunk] += landing[strip, chunk].astype(jnp.float32)

    for step in range(7):
        for chunk in range(2):
            for way in (1, -1):
                rank = strip if way == 1 else 7 - strip

                @pl.when(rank <= step)
                def _():
                    ahead = 7 - step + rank
                    chain(ahead if way == 1 else 7 - ahead, chunk, way).wait_send()

    for copy in copies.sent:
        copy.wait_send()


def pack_kernel(owner, frame, row, col, valid, crop, packed, cells, count, base):
    packed[...] = jnp.zeros_like(packed)

    def clear(i, _):
        count[i] = 0
        base[2 * i] = 0
        base[2 * i + 1] = 0
        return 0

    lax.fori_loop(0, 64, clear, 0)

    def put(k, _):
        @pl.when(valid[k] != 0)
        def _():
            name = owner[k]
            rank = count[name]
            count[name] = rank + 1
            slot = ((name // 16) * 2 + name % 2) * 16 + (name % 16) // 2 * 2 + rank
            base[slot] = frame[k] * 256 + row[k] * 16 + col[k]
            packed[slot] = crop[k]

        return 0

    lax.fori_loop(0, 64, put, 0)
    where = lax.broadcasted_iota(jnp.int32, (1, 128), 1)
    offset = (where % 64) // 8 * 16 + where % 8

    def mark(i, _):
        cells[pl.ds(i, 1), :] = offset + jnp.where(where < 64, base[2 * i], base[2 * i + 1])
        return 0

    lax.fori_loop(0, 64, mark, 0)


def place_kernel(crops, places, part):
    goal = pl.program_id(0)
    cell = lax.broadcasted_iota(jnp.int32, (512, 128), 0)
    summed = jnp.zeros((512, 256), jnp.float32)
    for pair in range(4):
        hits = [
            jnp.where(cell == places[2 * pair + i, pl.ds(goal, 1), :], 1.0, 0.0).astype(jnp.bfloat16)
            for i in range(2)
        ]
        summed += jnp.dot(
            jnp.concatenate(hits, 1),
            crops[0, 2 * pair : 2 * pair + 2].reshape(256, 256),
            preferred_element_type=jnp.float32,
        )
    part[0] = summed.astype(jnp.bfloat16)


def convolve(padded, kernel_taps, frames, rows, cols):
    width = kernel_taps.shape[-1]
    summed = jnp.zeros((frames * rows * cols, width), jnp.float32)
    for frame_off in range(3):
        windows = []
        for row_off in range(3):
            for col_off in range(3):
                windows.append(
                    padded[
                        frame_off : frame_off + frames,
                        row_off : row_off + rows,
                        col_off : col_off + cols,
                        :,
                    ]
                )
        stacked = jnp.concatenate(windows, -1).reshape(frames * rows * cols, 9 * width)
        tap_block = kernel_taps[frame_off * 9 : (frame_off + 1) * 9].reshape(9 * width, width)
        summed = summed + jnp.dot(stacked, tap_block, preferred_element_type=jnp.float32)
    return summed.reshape(frames, rows, cols, width)


def joined(ext, left, right, far_frames, far_there):
    rows = ext.shape[1]
    x, strip = lax.axis_index("ha"), lax.axis_index("wa")
    frame = lax.broadcasted_iota(jnp.int32, (4, rows, 1, 1), 0)
    row = lax.broadcasted_iota(jnp.int32, (4, rows, 1, 1), 1)
    there = (
        ((row > 0) | (x > 0))
        & ((row < rows - 1) | (x < 3))
        & (((frame < far_frames[0]) | (frame > far_frames[1])) | far_there)
    )
    zero = jnp.zeros((), jnp.bfloat16)
    padded = jnp.concatenate(
        [
            jnp.where(strip > 0, left[:, :rows, None, :], zero),
            ext,
            jnp.where(strip < 15, right[:, :rows, None, :], zero),
        ],
        2,
    )
    return jnp.where(there, padded, zero)


VM = functools.partial(pl.BlockSpec, memory_space=pltpu.VMEM)
SM = functools.partial(pl.BlockSpec, memory_space=pltpu.SMEM)
ANY = functools.partial(pl.BlockSpec, memory_space=pl.ANY)
DMA = pltpu.SemaphoreType.DMA


def per_device(
    features, conv_weight, down_weight, grad_out, crop_grad,
    crop_owner, crop_frame, crop_row, crop_col, crop_valid,
):
    frames, rows, cols, width = features.shape
    half_type, shape = jnp.bfloat16, jax.ShapeDtypeStruct
    packed, cells = pl.pallas_call(
        pack_kernel,
        out_shape=(shape((128, 64, width), half_type), shape((64, 128), jnp.int32)),
        in_specs=[SM()] * 5 + [VM()],
        out_specs=(VM(), VM()),
        scratch_shapes=[pltpu.SMEM((64,), jnp.int32), pltpu.SMEM((128,), jnp.int32)],
        compiler_params=pltpu.CompilerParams(vmem_limit_bytes=32 << 20),
    )(
        crop_owner[:, 0], crop_frame, crop_row, crop_col, crop_valid,
        crop_grad.reshape(64, 64, width),
    )
    ext_shape = shape((4, rows + 2, cols, width), half_type)
    side_shape = shape((4, 32, width), half_type)
    copies_a, copies_b = 48, 10
    ext, left, right, taps, crops, places = pl.pallas_call(
        gather_kernel,
        out_shape=(
            ext_shape, side_shape, side_shape,
            shape((16, 432, width), half_type),
            shape((8, 8, 128, width), half_type),
            shape((8, 8, 128), jnp.int32),
        ),
        in_specs=[VM(), VM(), ANY(), VM()],
        out_specs=(VM(), VM(), VM(), ANY(), ANY(), VM()),
        scratch_shapes=[
            pltpu.VMEM((2, rows, cols, width), half_type),
            pltpu.VMEM((2, 4, 32, width), half_type),
            pltpu.VMEM((2, 8, 128, width), half_type),
            pltpu.VMEM((8, 128, width), half_type),
            DMA((copies_a,)), DMA((copies_a,)), DMA((3,)),
        ],
        compiler_params=pltpu.CompilerParams(
            collective_id=0, has_side_effects=True, vmem_limit_bytes=32 << 20
        ),
    )(features, conv_weight, packed.reshape(8, 8, 128, width), cells.reshape(8, 8, 128))
    part = pl.pallas_call(
        place_kernel,
        grid=(8,),
        out_shape=shape((8, 512, width), half_type),
        in_specs=[pl.BlockSpec((1, 8, 128, width), lambda i: (i, 0, 0, 0)), VM()],
        out_specs=pl.BlockSpec((1, 512, width), lambda i: (i, 0, 0)),
    )(crops, places)
    slab = lax.axis_index("ta")
    kernel_taps = taps.reshape(27, width, width)
    padded = joined(ext, left, right, (0, 1), slab > 0)
    preact = convolve(padded, kernel_taps, frames, rows, cols)
    sigmoid_h = jax.nn.sigmoid(preact)
    section_out = (features.astype(jnp.float32) + preact * sigmoid_h).astype(jnp.bfloat16)
    down_mat = down_weight.reshape(4 * width, width)
    pooled = (
        section_out.reshape(frames, rows // 2, 2, cols // 2, 2, width)
        .transpose(0, 1, 3, 2, 4, 5)
        .reshape(-1, 4 * width)
    )
    reduced = (
        jnp.dot(pooled, down_mat, preferred_element_type=jnp.float32)
        .astype(jnp.bfloat16)
        .reshape(frames, rows // 2, cols // 2, width)
    )
    spread = jnp.dot(grad_out.reshape(-1, width), down_mat.T, preferred_element_type=jnp.float32)
    spread = (
        spread.reshape(frames, rows // 2, cols // 2, 2, 2, width)
        .transpose(0, 1, 3, 2, 4, 5)
        .reshape(frames, rows, cols, width)
    )
    grad_pre = (spread * sigmoid_h * (1.0 + preact * (1.0 - sigmoid_h))).astype(jnp.bfloat16)
    chain = pltpu.VMEM((8, 2, 256, width), half_type)
    ext, left, right, crop_terms = pl.pallas_call(
        scatter_kernel,
        out_shape=(
            ext_shape, side_shape, side_shape, shape((2, 256, width), jnp.float32),
        ),
        in_specs=[VM(), VM()],
        out_specs=(VM(), VM(), VM(), VM()),
        scratch_shapes=[
            pltpu.VMEM((2, rows, cols, width), half_type),
            pltpu.VMEM((2, 4, 32, width), half_type),
            chain, chain, chain, chain,
            DMA((copies_b,)), DMA((copies_b,)),
            DMA((8, 2)), DMA((8, 2)), DMA((8, 2)), DMA((8, 2)),
        ],
        compiler_params=pltpu.CompilerParams(
            collective_id=1, has_side_effects=True, vmem_limit_bytes=32 << 20
        ),
    )(grad_pre, part.reshape(8, 2, 256, width))
    flipped = jnp.transpose(kernel_taps[::-1], (0, 2, 1))
    back_pad = joined(ext, left, right, (2, 3), slab < 7)
    through = convolve(back_pad, flipped, frames, rows, cols)
    grad_in = (spread + through + crop_terms.reshape(frames, rows, cols, width)).astype(
        jnp.bfloat16
    )
    return (reduced, grad_in)


def solution(mesh):
    spread_all = ("ta", "ha", "wa")
    tile = P("ta", "ha", "wa", None)
    in_specs = (
        tile, P("wa", None), P(), tile, P(spread_all, None, None, None), P(spread_all, None),
        P(spread_all), P(spread_all), P(spread_all), P(spread_all),
    )
    return jax.shard_map(
        per_device, mesh=mesh, in_specs=in_specs, out_specs=(tile, tile), check_vma=False
    )
```

time: 449 us -> 193 us (0.43)
  the two profiles are of different devices: /device:TPU:29 before, /device:TPU:1 now
where the time goes in v1:
time: 193 us
  Pallas kernels  151 us (78%)
  local copies, waits for them, and re-layouts  33 us (17%)
  matrix products  5.83 us (3%)
  other arithmetic  2.07 us (1%)
    pallas_call x1, Pallas kernels, per_device(): pl.pallas_call(scatter_kernel, out_shape=(ext_shape, side_shape, side_sha...  70.9 us
    pallas_call x1, Pallas kernels, per_device(): pl.pallas_call(gather_kernel, out_shape=(ext_shape, side_shape, side_shap...  68.5 us
    unnamed x60, local copies, waits for them, and re-layouts  22.6 us
    pallas_call x1, Pallas kernels, per_device(): pl.pallas_call(place_kernel, grid=(8,), out_shape=shape((8, 512, width),...  7.72 us
    reshape x1, local copies, waits for them, and re-layouts, per_device(): kernel_taps = taps.reshape(27, width, width)  5.72 us
    dot_general x6, matrix products, convolve(): jnp.dot(stacked, tap_block, preferred_element_type=jnp.float32)  4.66 us

profile of v1, /device:TPU:1, one launch (start us, length us, event | category | flops | bytes accessed | tf_op | source)
XLA Modules:
  0.0 192.7 jit_solution(12977260648407283959)
XLA Ops:
  0.7 1.6 copy-done.5
  2.3 0.7 copy-done.10
  3.0 0.7 copy-done.11
  3.6 0.7 copy-done.12
  4.3 0.7 copy-done.13
  4.9 0.7 copy-done.14
  5.6 3.5 %shard_map.113 = (bf16[128,64,256]{2,1,0:T(8,128)(2,1)S(1)}, s32[64,128]{1,0:T(8,128)S(1)}) custom-call(s32[64]{0:T(128)S(1)} %bitcast.72, s32[64]{0:T(128)S(1)} %copy-done.11, s32[64]{0:T(128)S(1)} %copy-done.12, s32[64]{0:T(128)S(1)} %copy-done.13, s32[64]{0:T(128)S(1)} %copy-done.14, bf16[64,64,256]{2,1,0:T(8,128)(2,1)S(1)} %bitcast.69), custom_call_target="tpu_custom_call" | custom-call | tf_op jit(solution)/shard_map/pallas_call | solution.py:478
  9.1 0.9 copy-done.6
  10.0 0.9 copy-done.8
  11.0 68.5 %shard_map.114 = (bf16[4,18,16,256]{3,2,1,0:T(8,128)(2,1)S(1)}, bf16[4,32,256]{2,1,0:T(8,128)(2,1)S(1)}, bf16[4,32,256]{2,1,0:T(8,128)(2,1)S(1)}, bf16[16,432,25...) custom-call(bf16[2,16,16,256]{3,2,1,0:T(8,128)(2,1)S(1)} %copy-done.6, ...), custom_call_target="tpu_custom_call" | custom-call | tf_op jit(solution)/shard_map/pallas_call | solution.py:492
  79.5 1.7 copy-done.1
  81.2 2.0 %copy-done.4 = bf16[8,8,128,256]{3,2,1,0:T(8,128)(2,1)} copy-done((bf16[8,8,128,256]{3,2,1,0:T(8,128)(2,1)}, bf16[8,8,128,256]{3,2,1,0:T(8,128)(2,1)S(1)}, u32[]{:S(2)}) %copy-start.4) | copy-done | bytes 4194328
  83.2 0.6 copy-done.9
  83.8 0.1 copy.17
  83.9 0.1 copy.18
  84.0 0.1 broadcast_and_fusion
  84.1 0.4 maximum_select_fusion
  84.5 0.1 slice_dynamic-update-slice_fusion.35
  84.6 0.2 slice_dynamic-update-slice_fusion.34
  84.8 0.2 slice_dynamic-update-slice_fusion.33
  85.0 0.1 slice_dynamic-update-slice_fusion.32
  85.0 0.2 slice_dynamic-update-slice_fusion.31
  85.3 0.2 slice_dynamic-update-slice_fusion.30
  85.5 0.1 slice_dynamic-update-slice_fusion.29
  85.5 0.2 slice_dynamic-update-slice_fusion.28
  85.7 0.2 slice_dynamic-update-slice_fusion.27
  86.0 1.5 copy-done.2
  87.5 0.4 fusion.3
  87.8 0.8 fusion.4
  88.6 0.8 convolution_add_fusion.3
  89.4 0.8 convolution_add_fusion.2
  90.3 0.3 convolution_bitcast_fusion
  90.6 0.3 copy.20
  90.9 0.4 reshape.168
  91.2 0.3 multiply_convert_fusion
  91.5 7.7 %shard_map.115 = bf16[8,512,256]{2,1,0:T(8,128)(2,1)} custom-call(bf16[8,8,128,256]{3,2,1,0:T(8,128)(2,1)} %copy-done.4, s32[8,8,128]{2,1,0:T(8,128)} %copy-done.9), custom_call_target="tpu_custom_call" | custom-call | tf_op jit(solution)/shard_map/pallas_call | solution.py:513
  99.3 1.6 copy-done.3
  100.8 70.9 %shard_map.116 = (bf16[4,18,16,256]{3,2,1,0:T(8,128)(2,1)S(1)}, bf16[4,32,256]{2,1,0:T(8,128)(2,1)S(1)}, bf16[4,32,256]{2,1,0:T(8,128)(2,1)S(1)}, f32[2,256,256]{2,1,0:T(8,128)S(1)}) custom-call(bf16[2,16,16,256]{3,2,1,0:T(8,128)(2,1)S(1)} %get-tuple-element.86.tile, bf16[8,2,256,256]{3,2,1,0:T(8,128)(2,1)S(1)} %bitcast.67), custom_call_target="tpu_custom_call" | custom-call | tf_op jit(solution)/shard_map/pallas_call | solution.py:545
  172.0 0.4 maximum_select_fusion.1
  172.4 0.1 slice_dynamic-update-slice_fusion.8
  172.4 0.2 slice_dynamic-update-slice_fusion.7
  172.7 0.2 slice_dynamic-update-slice_fusion.6
  172.9 0.1 slice_dynamic-update-slice_fusion.5
  172.9 0.2 slice_dynamic-update-slice_fusion.4
  173.1 0.2 slice_dynamic-update-slice_fusion.3
  173.3 0.1 slice_dynamic-update-slice_fusion.2
  173.4 0.2 slice_dynamic-update-slice_fusion.1
  173.6 0.2 slice_dynamic-update-slice_fusion
  173.8 1.4 copy-done.15
  175.2 1.5 copy-done.17
  176.7 0.8 copy-done.20
  177.5 5.7 %copy.23 = bf16[27,256,256]{1,2,0:T(8,128)(2,1)} copy(bf16[27,256,256]{2,1,0:T(8,128)(2,1)} %bitcast.65) | data formatting | bytes 7077888 | tf_op jit(solution)/shard_map/reshape | solution.py:521
  183.2 2.4 %reverse_bitcast_fusion = bf16[27,256,256]{2,1,0:T(8,128)(2,1)S(1)} fusion(bf16[27,256,256]{1,2,0:T(8,128)(2,1)} %copy.23), kind=kLoop, calls=%fused_computation | loop fusion | bytes 7077888 | tf_op jit(solution)/shard_map/transpose | solution.py:563
  185.6 0.2 fusion.2
  185.8 1.4 copy-done.21
  187.2 0.8 fusion.5
  188.0 0.8 convolution_add_fusion.1
  188.8 0.9 copy-done.16
  189.7 0.8 convolution_add_fusion
  190.5 0.8 add_convert_fusion
  191.3 0.1 reshape.164
  191.4 0.2 copy.27
  191.6 0.2 reshape.165
  191.8 0.9 convolution_convert_fusion
  (33 shorter events, 0.2 us)
Async XLA Ops:
  0.6 89.6 %copy-start = (bf16[2,2,256,256]{3,2,1,0:T(8,128)(2,1)S(1)}, bf16[2,2,256,256]{3,2,1,0:T(8,128)(2,1)}, u32[]{:S(2)}) copy-start(bf16[2,2,256,256]{3,2,1,0:T(8,128)(2,1)} %param.12) | copy-start | bytes 1572868
  0.6 1.6 copy-start.5
  2.3 0.7 copy-start.10
  3.0 0.7 copy-start.11
  3.6 0.7 copy-start.12
  4.3 0.7 copy-start.13
  4.9 0.7 copy-start.14
  9.1 1.0 copy-start.6
  10.0 0.9 copy-start.8
  79.5 1.7 copy-start.1
  81.2 2.0 %copy-start.4 = (bf16[8,8,128,256]{3,2,1,0:T(8,128)(2,1)}, bf16[8,8,128,256]{3,2,1,0:T(8,128)(2,1)S(1)}, u32[]{:S(2)}) copy-start(bf16[8,8,128,256]{3,2,1,0:T(8,128)(2,1)S(1)} %get-tuple-element.20.crops) | copy-start | bytes 12582916
  83.2 0.6 copy-start.9
  85.5 2.0 %copy-start.2 = (bf16[16,432,256]{2,1,0:T(8,128)(2,1)S(1)}, bf16[16,432,256]{2,1,0:T(8,128)(2,1)}, u32[]{:S(2)}) copy-start(bf16[16,432,256]{2,1,0:T(8,128)(2,1)} %copy-done.1) | copy-start | bytes 10616836
  89.4 0.8 copy-start.19
  90.2 1.0 copy-start.7
  99.3 1.6 copy-start.3
  173.8 1.4 copy-start.15
  175.2 1.5 copy-start.17
  175.2 2.2 %copy-start.20 = (bf16[2,16,16,2304]{3,2,1,0:T(8,128)(2,1)}, bf16[2,16,16,2304]{3,2,1,0:T(8,128)(2,1)S(1)}, u32[]{:S(2)}) copy-start(bf16[2,16,16,2304]{3,2,1,0:T(8,128)(2,1)S(1)} %get-tuple-element.34) | copy-start | bytes 7077892
  185.6 1.7 copy-start.21
  185.8 2.2 %copy-start.18 = (bf16[2,16,16,2304]{3,2,1,0:T(8,128)(2,1)S(1)}, bf16[2,16,16,2304]{3,2,1,0:T(8,128)(2,1)}, u32[]{:S(2)}) copy-start(bf16[2,16,16,2304]{3,2,1,0:T(8,128)(2,1)} %copy-done.17) | copy-start | bytes 7077892
  188.0 1.7 copy-start.16

commit v2 on v1

v2 whole, which is shorter than its diff:
```python
import functools

import jax
import jax.numpy as jnp
from jax import lax
from jax.experimental import pallas as pl
from jax.experimental.pallas import tpu as pltpu
from jax.sharding import PartitionSpec as P

MESH = pl.DeviceIdType.MESH
CAP = 2


def place():
    slab, x, strip = lax.axis_index("ta"), lax.axis_index("ha"), lax.axis_index("wa")
    return slab // 2, (slab % 2) * 8 + strip // 2, x, strip % 2


def at(y, z, x, core):
    y, z, x = (y + 4) % 4, (z + 16) % 16, (x + 4) % 4
    return (y * 2 + z // 8, x, (z % 8) * 2 + core)


class Copies:
    def __init__(self, send_sems, recv_sems):
        self.send_sems, self.recv_sems, self.used, self.sent = send_sems, recv_sems, 0, []

    def make(self, src, dst, device):
        slot = self.used
        self.used += 1
        return pltpu.make_async_remote_copy(
            src_ref=src,
            dst_ref=dst,
            send_sem=self.send_sems.at[slot],
            recv_sem=self.recv_sems.at[slot],
            device_id=device,
            device_id_type=MESH,
        )

    def start(self, src, dst, device):
        copy = self.make(src, dst, device)
        copy.start()
        self.sent.append(copy)
        return copy


def greet(devices):
    barrier = pltpu.get_barrier_semaphore()
    for device in devices:
        pl.semaphore_signal(barrier, inc=1, device_id=device, device_id_type=MESH)
    pl.semaphore_wait(barrier, len(devices))


def edge_columns(ext, edge, frame):
    rows, cols, width = ext.shape[1:]
    flat = ext[frame].reshape(rows * cols, width)
    row = lax.broadcasted_iota(jnp.int32, (edge.shape[2], rows * cols), 0)
    cell = lax.broadcasted_iota(jnp.int32, (edge.shape[2], rows * cols), 1)
    for side, col in ((0, 0), (1, cols - 1)):
        pick = jnp.where(cell == row * cols + col, 1.0, 0.0).astype(jnp.bfloat16)
        edge[side, frame] = jnp.dot(pick, flat, preferred_element_type=jnp.float32).astype(
            jnp.bfloat16
        )


class Halo:
    def __init__(self, copies, tile, ext, left, right, relay, edge, own, other, step):
        self.copies, self.tile, self.ext, self.left, self.right = copies, tile, ext, left, right
        self.relay, self.edge, self.own, self.other, self.step = relay, edge, own, other, step

    def first(self):
        y, z, x, core = place()
        self.up = self.copies.start(self.tile.at[0], self.relay.at[0], at(y, z + 4, x, core))
        self.down = self.copies.start(self.tile.at[1], self.relay.at[1], at(y, z - 4, x, core))

    def own_rows(self):
        y, z, x, core = place()
        ext, own = self.ext, self.own
        rows = self.tile.shape[1]
        self.rows_own = [
            self.copies.start(
                self.tile.at[:, pl.ds(rows - 1, 1)],
                ext.at[pl.ds(own, 2), pl.ds(0, 1)],
                at(y, z, x + 1, core),
            ),
            self.copies.start(
                self.tile.at[:, pl.ds(0, 1)],
                ext.at[pl.ds(own, 2), pl.ds(rows + 1, 1)],
                at(y, z, x - 1, core),
            ),
        ]
        ext[own : own + 2, 1 : rows + 1] = self.tile[...]

    def forward(self):
        y, z, x, core = place()
        rows = self.tile.shape[1]
        self.far = []
        for frame, copy, turn in ((0, self.up, 4), (1, self.down, -4)):
            source_hi = ((z - turn + 16) % 16) // 8
            y_to = y + source_hi if self.step == 1 else y - 1 + source_hi
            copy.wait_recv()
            self.far.append(
                self.copies.start(
                    self.relay.at[frame],
                    self.ext.at[self.other + frame, pl.ds(1, rows)],
                    at(y_to, z + turn, x, core),
                )
            )

    def near_columns(self):
        for copy in self.rows_own:
            copy.wait_recv()
        for frame in range(2):
            edge_columns(self.ext, self.edge, self.own + frame)

    def far_rows(self):
        y, z, x, core = place()
        ext, other = self.ext, self.other
        rows = self.tile.shape[1]
        for copy in self.far:
            copy.wait_recv()
        self.borders = [
            self.copies.start(
                ext.at[pl.ds(other, 2), pl.ds(rows, 1)],
                ext.at[pl.ds(other, 2), pl.ds(0, 1)],
                at(y, z, x + 1, core),
            ),
            self.copies.start(
                ext.at[pl.ds(other, 2), pl.ds(1, 1)],
                ext.at[pl.ds(other, 2), pl.ds(rows + 1, 1)],
                at(y, z, x - 1, core),
            ),
        ]

    def finish(self):
        y, z, x, core = place()
        for copy in self.borders:
            copy.wait_recv()
        for frame in range(2):
            edge_columns(self.ext, self.edge, self.other + frame)
        sides = [
            self.copies.start(self.edge.at[1], self.left, at(y, z + core, x, 1 - core)),
            self.copies.start(self.edge.at[0], self.right, at(y, z - 1 + core, x, 1 - core)),
        ]
        for copy in sides:
            copy.wait_recv()


def halo_partners():
    y, z, x, core = place()
    return [
        at(y, z + 4, x, core),
        at(y, z - 4, x, core),
        at(y + 1, z + 4, x, core),
        at(y - 1, z - 4, x, core),
        at(y + 1, z - 4, x, core),
        at(y - 1, z + 4, x, core),
        at(y, z, x + 1, core),
        at(y, z, x - 1, core),
        at(y, z, x, 1 - core),
        at(y, z + 1, x, core),
        at(y, z - 1, x, core),
        at(y, z - 1 + 2 * core, x, 1 - core),
    ]


def table_kernel(owner, frame, row, col, valid, source, cells, index, count, base, sems):
    moves = [
        pltpu.make_async_copy(ref, index.at[i], sems.at[i])
        for i, ref in enumerate((owner, frame, row, col, valid))
    ]
    for move in moves:
        move.start()

    def clear(i, _):
        count[i] = 0
        for rank in range(2):
            base[2 * i + rank] = 0
            source[2 * i + rank] = 64
        return 0

    lax.fori_loop(0, 64, clear, 0)
    for move in moves:
        move.wait()

    def put(k, _):
        @pl.when(index[4, k] != 0)
        def _():
            name = index[0, k]
            rank = count[name]
            count[name] = rank + 1
            deep = (name % 16) // 2
            spot = jnp.where(deep < 4, 2 * deep + 1, 2 * (7 - deep))
            slot = ((name // 16) * 2 + name % 2) * 16 + spot * 2 + rank
            base[slot] = index[1, k] * 256 + index[2, k] * 16 + index[3, k]
            source[slot] = k

        return 0

    lax.fori_loop(0, 64, put, 0)
    where = lax.broadcasted_iota(jnp.int32, (1, 128), 1)
    offset = (where % 64) // 8 * 16 + where % 8

    def mark(i, _):
        cells[pl.ds(i, 1), :] = offset + jnp.where(where < 64, base[2 * i], base[2 * i + 1])
        return 0

    lax.fori_loop(0, 64, mark, 0)


def gather_kernel(
    tile, shard, source, cells, crop_grad, ext, left, right, taps, total,
    relay, edge, crop, packed, crops, places, cross, part,
    in_up, in_down, out_up, out_down,
    send_sems, recv_sems, local_sems, up_send, up_recv, down_send, down_recv,
):
    y, z, x, core = place()
    strip = z % 8
    copies = Copies(send_sems, recv_sems)
    crop_in = pltpu.make_async_copy(crop_grad, crop.at[pl.ds(0, 64)], local_sems.at[1])
    crop_in.start()
    own_shard = pltpu.make_async_copy(shard, taps.at[strip * 2 + core], local_sems.at[0])
    own_shard.start()
    crop[64] = jnp.zeros_like(crop[64])
    greet(
        halo_partners()
        + [
            at(y, z, x + 1, 1 - core),
            at(y, z, x - 1, 1 - core),
            at(y, z, x + 2, core),
            at(y, z, x + 2, 1 - core),
            at(y + 1, z, x, core),
            at(y - 1, z, x, core),
        ]
    )
    halo = Halo(copies, tile, ext, left, right, relay, edge, 2, 0, 1)
    half = pl.ds(pl.multiple_of((y % 2) * 128, 128), 128)
    mine = x * 2 + core
    turn = 1 - 2 * core

    def lane(offset):
        return ((strip + offset + 8) % 8) * 2 + core

    ring = {}
    for way in (1, -1):
        ring[way] = copies.start(
            shard.at[:, half], taps.at[lane(0), :, half], at(y, z + way, x, core)
        )
    crop_in.wait()

    def pack(dest):
        def fill(i, _):
            packed[dest, i // 4, i // 2 % 2, pl.ds(i % 2 * 64, 64)] = crop[source[dest * 16 + i]]
            return 0

        lax.fori_loop(0, 16, fill, 0)

    across = [((x + 2) % 4) * 2 + (core + flip) % 2 for flip in range(2)]
    near = [
        (away, flip, ((x + away + 4) % 4) * 2 + (core + flip) % 2)
        for away in (1, -1)
        for flip in range(2)
    ]

    def cross_send(group):
        return [
            copies.start(
                packed.at[across[flip], group], cross.at[flip, group], at(y, z, x + turn, core)
            )
            for flip in range(2)
        ]

    def cross_pass(arriving, group):
        origin = ((x - turn + 4) % 4) * 2 + core
        passed = []
        for flip in range(2):
            arriving[flip].wait_recv()
            passed.append(
                copies.start(
                    cross.at[flip, group],
                    crops.at[group, :, origin],
                    at(y, z, x + turn, (core + flip) % 2),
                )
            )
        return passed

    def near_send(group):
        return [
            copies.start(
                packed.at[dest, group],
                crops.at[group, :, mine],
                at(y, z, x + away, (core + flip) % 2),
            )
            for away, flip, dest in near
        ] + [
            copies.start(
                packed.at[x * 2 + 1 - core, group],
                crops.at[group, :, mine],
                at(y, z, x, 1 - core),
            )
        ]

    crossing, crossed, nearby = {}, {}, {}
    for dest in across:
        pack(dest)
    crossing[0] = cross_send(0)
    for _, _, dest in near:
        pack(dest)
    pack(x * 2 + 1 - core)
    nearby[0] = near_send(0)
    crossing[1] = cross_send(1)
    halo.first()
    halo.own_rows()
    got = []
    for away in (1, 2, 3):
        for flip in range(2):
            to = (core + flip) % 2
            got.append(
                copies.start(
                    cells.at[((x + away) % 4) * 2 + to], places.at[mine], at(y, z, x + away, to)
                )
            )
    got.append(
        copies.start(cells.at[x * 2 + 1 - core], places.at[mine], at(y, z, x, 1 - core))
    )
    rest = [copies.start(shard, taps.at[lane(0)], at(y, z, x, 1 - core))]
    places[mine] = cells[mine]

    def keep(i, _):
        crops[i // 4, i // 2 % 2, mine, pl.ds(i % 2 * 64, 64)] = crop[source[mine * 16 + i]]
        return 0

    lax.fori_loop(0, 16, keep, 0)

    swaps = {}

    def swap(offset, y_to):
        piece = taps.at[lane(offset), :, half]
        swaps[offset] = copies.start(piece, piece, at(y_to, z, x, core))

    def ring_step(step):
        for way in (1, -1):
            ring[way].wait_recv()
            offset = -way * step
            if step < 3:
                piece = taps.at[lane(offset), :, half]
                ring[way] = copies.start(piece, piece, at(y, z + way, x, core))
            swap(offset, y + way)

    def whole(offset):
        swaps[offset].wait_recv()
        shard_all = taps.at[lane(offset)]
        rest.append(copies.start(shard_all, shard_all, at(y, z, x, 1 - core)))

    cell = lax.broadcasted_iota(jnp.int32, (512, 128), 0)

    def settle(group):
        for copy in nearby[group] + crossed[group] + (got if group == 0 else []):
            copy.wait_recv()
        for i in range(2):
            goal = 7 - group if i == 0 else group
            part[goal] = jnp.zeros_like(part[goal])

            def add(pair, _):
                hits = [
                    jnp.where(cell == places[2 * pair + j, 2 * group + i][None, :], 1.0, 0.0).astype(
                        jnp.bfloat16
                    )
                    for j in range(2)
                ]
                part[goal] += jnp.dot(
                    jnp.concatenate(hits, 1),
                    crops[group, i, pl.ds(2 * pair, 2)].reshape(256, 256),
                    preferred_element_type=jnp.float32,
                )
                return 0

            lax.fori_loop(0, 4, add, 0)

    def chain(goal, chunk, way):
        landing, leaving, sends, recvs = (
            (in_up, out_up, up_send, up_recv) if way == 1 else (in_down, out_down, down_send, down_recv)
        )
        return pltpu.make_async_remote_copy(
            src_ref=leaving.at[goal, chunk],
            dst_ref=landing.at[goal, chunk],
            send_sem=sends.at[goal, chunk],
            recv_sem=recvs.at[goal, chunk],
            device_id=at(y, z + way, x, core),
            device_id_type=MESH,
        )

    def turn_of(step, way):
        rank = strip if way == 1 else 7 - strip
        turn_at = step - rank + 16
        late = (turn_at - 16 + 32) % 32
        odd = late % 2
        ahead = (1 - odd) * (7 - late // 2) + odd * (late // 2)
        busy = (late < 8) & (late != 1) & (rank < ahead)
        return rank, (ahead if way == 1 else 7 - ahead), busy

    def advance(step, chunk, way):
        rank, goal, busy = turn_of(step, way)
        landing, leaving = (in_up, out_up) if way == 1 else (in_down, out_down)

        @pl.when(busy)
        def _():
            copy = chain(goal, chunk, way)
            mid = part[goal, pl.ds(chunk * 256, 256)]

            @pl.when(rank > 0)
            def _():
                copy.wait_recv()
                leaving[goal, chunk] = (mid + landing[goal, chunk].astype(jnp.float32)).astype(
                    jnp.bfloat16
                )

            @pl.when(rank == 0)
            def _():
                leaving[goal, chunk] = mid.astype(jnp.bfloat16)

            copy.start()

    def slot(step):
        for chunk in range(2):
            for way in (1, -1):
                advance(step, chunk, way)

    ring_step(1)
    crossed[0] = cross_pass(crossing[0], 0)
    nearby[1] = near_send(1)
    crossing[2] = cross_send(2)
    ring_step(2)
    settle(0)
    slot(0)
    ring_step(3)
    far = taps.at[lane(4), :, half]
    piece = taps.at[lane(-3 * turn), :, half]
    ring_last = copies.start(piece, piece, at(y, z + turn, x, core))
    crossed[1] = cross_pass(crossing[1], 1)
    nearby[2] = near_send(2)
    crossing[3] = cross_send(3)
    halo.forward()
    slot(1)
    ring_last.wait_recv()
    swaps[4] = copies.start(far, far, at(y + turn, z, x, core))
    for offset in (1, -1, 2, -2):
        whole(offset)
    settle(1)
    slot(2)
    crossed[2] = cross_pass(crossing[2], 2)
    nearby[3] = near_send(3)
    slot(3)
    for offset in (3, -3, 4):
        whole(offset)
    settle(2)
    slot(4)
    crossed[3] = cross_pass(crossing[3], 3)
    slot(5)
    settle(3)
    slot(6)
    halo.near_columns()
    slot(7)
    halo.far_rows()
    slot(8)
    halo.finish()
    slot(9)
    assert copies.used == SENDS, copies.used
    for chunk in range(2):
        total[chunk] = part[strip, pl.ds(chunk * 256, 256)]
        for way in (1, -1):
            landing = in_up if way == 1 else in_down

            @pl.when((strip if way == 1 else 7 - strip) > 0)
            def _():
                chain(strip, chunk, way).wait_recv()
                total[chunk] += landing[strip, chunk].astype(jnp.float32)

    for copy in rest:
        copy.wait_recv()
    own_shard.wait()
    for step in range(10):
        for chunk in range(2):
            for way in (1, -1):
                rank, goal, busy = turn_of(step, way)

                @pl.when(busy)
                def _():
                    chain(goal, chunk, way).wait_send()

    for copy in copies.sent:
        copy.wait_send()


SENDS = 75


def return_kernel(tile, ext, left, right, relay, edge, send_sems, recv_sems):
    copies = Copies(send_sems, recv_sems)
    greet(halo_partners())
    halo = Halo(copies, tile, ext, left, right, relay, edge, 0, 2, -1)
    halo.first()
    halo.own_rows()
    halo.forward()
    halo.near_columns()
    halo.far_rows()
    halo.finish()
    for copy in copies.sent:
        copy.wait_send()


def ones_where(hit):
    return jnp.where(hit, 1.0, 0.0).astype(jnp.bfloat16)


def exact(pick, rows):
    return jnp.dot(pick, rows, preferred_element_type=jnp.float32)


def widen(ext, left, right, wide, far, far_there):
    _, _, x, _ = place()
    strip = lax.axis_index("wa")
    cell = lax.broadcasted_iota(jnp.int32, (288, 288), 0)
    other = lax.broadcasted_iota(jnp.int32, (288, 288), 1)
    back = ones_where((other == cell - 1) & (cell % 16 != 0))
    ahead = ones_where((other == cell + 1) & (cell % 16 != 15))
    cell = lax.broadcasted_iota(jnp.int32, (288, 32), 0)
    other = lax.broadcasted_iota(jnp.int32, (288, 32), 1)
    from_left = ones_where(cell == other * 16 + jnp.where(strip > 0, 0, 4096))
    from_right = ones_where(cell == other * 16 + 15 + jnp.where(strip < 15, 0, 4096))
    row = lax.broadcasted_iota(jnp.int32, (288, 256), 0) // 16
    low, high = jnp.where(x > 0, 0, 1), jnp.where(x < 3, 17, 16)
    for frame in range(4):
        least = jnp.where(far_there, low, 99) if frame in far else low
        there = (row >= least) & (row <= high)
        flat = ext[frame].reshape(288, 256)
        parts = (
            exact(back, flat) + exact(from_left, left[frame]),
            flat.astype(jnp.float32),
            exact(ahead, flat) + exact(from_right, right[frame]),
        )
        for shift, value in enumerate(parts):
            wide[frame, :, :, 256 * shift : 256 * shift + 256] = (
                jnp.where(there, value, 0.0).astype(jnp.bfloat16).reshape(18, 16, 256)
            )


NT = (((1,), (1,)), ((), ()))


def forward_kernel(ext, left, right, taps, down, grad_out, reduced, grad_pre, spread, wide):
    widen(ext, left, right, wide, (0, 1), lax.axis_index("ta") > 0)
    preact = jnp.zeros((512, 256), jnp.float32)
    for a in range(3):
        for b in range(3):
            preact += jnp.dot(
                wide[a : a + 2, b : b + 16].reshape(512, 768),
                taps[a * 3 + b],
                preferred_element_type=jnp.float32,
            )
    sig = jax.nn.sigmoid(preact)
    own = ext[2:4, 1:17].reshape(512, 256).astype(jnp.float32)
    section = (own + preact * sig).astype(jnp.bfloat16)
    small = lax.broadcasted_iota(jnp.int32, (128, 512), 0)
    large = lax.broadcasted_iota(jnp.int32, (128, 512), 1)
    first = small // 64 * 256 + small // 8 % 8 * 32 + small % 8 * 2
    pooled = [
        exact(ones_where(large == first + p * 16 + q), section).astype(jnp.bfloat16)
        for p in range(2)
        for q in range(2)
    ]
    reduced[...] = jnp.dot(
        jnp.concatenate(pooled, 1), down[...].reshape(1024, 256), preferred_element_type=jnp.float32
    ).astype(jnp.bfloat16)
    large = lax.broadcasted_iota(jnp.int32, (512, 128), 0)
    small = lax.broadcasted_iota(jnp.int32, (512, 128), 1)
    over = ones_where(small == large // 256 * 64 + large // 32 % 8 * 8 + large // 2 % 8)
    repeated = exact(over, grad_out[...]).astype(jnp.bfloat16)
    cell = lax.broadcasted_iota(jnp.int32, (512, 256), 0)
    kind = cell // 16 % 2 * 2 + cell % 2
    back = jnp.zeros((512, 256), jnp.float32)
    for which in range(4):
        back = jnp.where(
            kind == which,
            lax.dot_general(repeated, down[which], NT, preferred_element_type=jnp.float32),
            back,
        )
    spread[...] = back
    grad_pre[...] = (back * sig * (1.0 + preact * (1.0 - sig))).astype(jnp.bfloat16)


def backward_kernel(ext, left, right, taps, spread, total, grad_in, wide):
    widen(ext, left, right, wide, (2, 3), lax.axis_index("ta") < 7)
    summed = spread[...] + total[...].reshape(512, 256)
    for a in range(3):
        for b in range(3):
            for c in range(3):
                summed += lax.dot_general(
                    wide[2 - a : 4 - a, 2 - b : 18 - b, :, 256 * (2 - c) : 256 * (3 - c)].reshape(
                        512, 256
                    ),
                    taps[(a * 3 + b) * 3 + c],
                    NT,
                    preferred_element_type=jnp.float32,
                )
    grad_in[...] = summed.astype(jnp.bfloat16)


VM = functools.partial(pl.BlockSpec, memory_space=pltpu.VMEM)
SM = functools.partial(pl.BlockSpec, memory_space=pltpu.SMEM)
ANY = functools.partial(pl.BlockSpec, memory_space=pl.ANY)
DMA = pltpu.SemaphoreType.DMA


def per_device(
    features, conv_weight, down_weight, grad_out, crop_grad,
    crop_owner, crop_frame, crop_row, crop_col, crop_valid,
):
    frames, rows, cols, width = features.shape
    half_type, shape = jnp.bfloat16, jax.ShapeDtypeStruct
    source, cells = pl.pallas_call(
        table_kernel,
        out_shape=(shape((128,), jnp.int32), shape((64, 128), jnp.int32)),
        in_specs=[ANY()] * 5,
        out_specs=(SM(), VM()),
        scratch_shapes=[
            pltpu.SMEM((5, 64), jnp.int32),
            pltpu.SMEM((64,), jnp.int32),
            pltpu.SMEM((128,), jnp.int32),
            DMA((5,)),
        ],
    )(crop_owner[:, 0], crop_frame, crop_row, crop_col, crop_valid)
    ext_shape = shape((4, rows + 2, cols, width), half_type)
    side_shape = shape((4, 32, width), half_type)
    relay = pltpu.VMEM((2, rows, cols, width), half_type)
    edge = pltpu.VMEM((2, 4, 32, width), half_type)
    chain = pltpu.VMEM((8, 2, 256, width), half_type)
    ext, left, right, taps, total = pl.pallas_call(
        gather_kernel,
        out_shape=(
            ext_shape, side_shape, side_shape,
            shape((16, 432, width), half_type),
            shape((2, 256, width), jnp.float32),
        ),
        in_specs=[VM(), VM(), SM(), VM(), ANY()],
        out_specs=(VM(), VM(), VM(), ANY(), VM()),
        scratch_shapes=[
            relay, edge,
            pltpu.VMEM((65, 64, width), half_type),
            pltpu.VMEM((8, 4, 2, 128, width), half_type),
            pltpu.VMEM((4, 2, 8, 128, width), half_type),
            pltpu.VMEM((8, 8, 128), jnp.int32),
            pltpu.VMEM((2, 4, 2, 128, width), half_type),
            pltpu.VMEM((8, 512, width), jnp.float32),
            chain, chain, chain, chain,
            DMA((SENDS,)), DMA((SENDS,)), DMA((2,)),
            DMA((8, 2)), DMA((8, 2)), DMA((8, 2)), DMA((8, 2)),
        ],
        compiler_params=pltpu.CompilerParams(
            collective_id=0, has_side_effects=True, vmem_limit_bytes=40 << 20
        ),
    )(features, conv_weight, source, cells.reshape(8, 8, 128), crop_grad.reshape(64, 64, width))
    wide = pltpu.VMEM((4, rows + 2, cols, 3 * width), half_type)
    roomy = pltpu.CompilerParams(vmem_limit_bytes=32 << 20)
    cells_all = frames * rows * cols
    reduced, grad_pre, spread = pl.pallas_call(
        forward_kernel,
        out_shape=(
            shape((cells_all // 4, width), half_type),
            shape((cells_all, width), half_type),
            shape((cells_all, width), jnp.float32),
        ),
        in_specs=[VM()] * 6,
        out_specs=(VM(), VM(), VM()),
        scratch_shapes=[wide],
        compiler_params=roomy,
    )(
        ext, left, right, taps.reshape(9, 3 * width, width),
        down_weight.reshape(4, width, width), grad_out.reshape(-1, width),
    )
    ext, left, right = pl.pallas_call(
        return_kernel,
        out_shape=(ext_shape, side_shape, side_shape),
        in_specs=[VM()],
        out_specs=(VM(), VM(), VM()),
        scratch_shapes=[relay, edge, DMA((10,)), DMA((10,))],
        compiler_params=pltpu.CompilerParams(
            collective_id=1, has_side_effects=True, vmem_limit_bytes=32 << 20
        ),
    )(grad_pre.reshape(frames, rows, cols, width))
    grad_in = pl.pallas_call(
        backward_kernel,
        out_shape=shape((cells_all, width), half_type),
        in_specs=[VM()] * 6,
        out_specs=VM(),
        scratch_shapes=[wide],
        compiler_params=roomy,
    )(ext, left, right, taps.reshape(27, width, width), spread, total)
    return (
        reduced.reshape(frames, rows // 2, cols // 2, width),
        grad_in.reshape(frames, rows, cols, width),
    )


def solution(mesh):
    spread_all = ("ta", "ha", "wa")
    tile = P("ta", "ha", "wa", None)
    in_specs = (
        tile, P("wa", None), P(), tile, P(spread_all, None, None, None), P(spread_all, None),
        P(spread_all), P(spread_all), P(spread_all), P(spread_all),
    )
    return jax.shard_map(
        per_device, mesh=mesh, in_specs=in_specs, out_specs=(tile, tile), check_vma=False
    )
```

time: 193 us -> 166 us (0.86)
  local copies, waits for them, and re-layouts: 33 us -> 6.76 us
  Pallas kernels: 151 us -> 157 us
  matrix products: 5.83 us -> 0 us
  other arithmetic: 2.07 us -> 0 us
    pallas_call x1, Pallas kernels: 68.5 us -> 99.5 us  [per_device(): pl.pallas_call(gather_kernel, out_shape=(ext_shape, side_shape, side_shap...]
    pallas_call x3 -> x4, Pallas kernels: 82.1 us -> 57.3 us  [the longest x1 44.9 us: per_device(): pl.pallas_call(return_kernel, out_shape=(ext_shape, side_shape, side_shap...]
    unnamed x60 -> x14, local copies, waits for them, and re-layouts: 22.6 us -> 6.76 us
    reshape x5 -> x0, local copies, waits for them, and re-layouts: 6.55 us -> none  [the longest x1 5.72 us: per_device(): kernel_taps = taps.reshape(27, width, width)]
    dot_general x8 -> x0, matrix products: 5.83 us -> none  [the longest x6 4.66 us: convolve(): jnp.dot(stacked, tap_block, preferred_element_type=jnp.float32)]
    transpose x2 -> x0, local copies, waits for them, and re-layouts: 2.65 us -> none  [the longest x1 2.37 us: per_device(): flipped = jnp.transpose(kernel_taps[::-1], (0, 2, 1))]
where the time goes in v2:
time: 166 us; the launch traced here: 164 us
  Pallas kernels  157 us (95%)
  local copies, waits for them, and re-layouts  6.76 us (4%)
    pallas_call x1, Pallas kernels, per_device(): pl.pallas_call(gather_kernel, out_shape=(ext_shape, side_shape, side_shap...  99.5 us
    pallas_call x1, Pallas kernels, per_device(): pl.pallas_call(return_kernel, out_shape=(ext_shape, side_shape, side_shap...  44.9 us
    unnamed x14, local copies, waits for them, and re-layouts  6.76 us
    pallas_call x1, Pallas kernels, per_device(): pl.pallas_call(forward_kernel, out_shape=(shape((cells_all // 4, width),...  4.67 us
    pallas_call x1, Pallas kernels, per_device(): pl.pallas_call(table_kernel, out_shape=(shape((128,), jnp.int32), shape((...  4.12 us
    pallas_call x1, Pallas kernels, per_device(): pl.pallas_call(backward_kernel, out_shape=shape((cells_all, width), half_...  3.61 us

profile of v2, /device:TPU:1, one launch (start us, length us, event | category | flops | bytes accessed | tf_op | source)
XLA Modules:
  0.0 164.2 jit_solution(2385380007703115592)
XLA Ops:
  0.6 4.1 %shard_map.113 = (s32[128]{0:T(128)}, s32[64,128]{1,0:T(8,128)}) custom-call(s32[64]{0:T(128)} %bitcast.18, s32[64]{0:T(128)} %frame.1, s32[64]{0:T(128)} %row.1, s32[64]{0:T(128)} %col.1, s32[64]{0:T(128)} %valid.1), custom_call_target="tpu_custom_call" | custom-call | tf_op jit(solution)/shard_map/pallas_call | solution.py:621
  4.8 0.0 copy-start
  4.8 1.6 copy-done
  6.4 0.0 copy-start.2
  6.4 0.9 copy-done.2
  7.3 0.0 copy-start.3
  7.3 0.9 copy-done.3
  8.2 0.0 copy-start.5
  8.2 0.8 copy-done.5
  9.0 0.0 copy-start.6
  9.0 0.7 copy-done.6
  9.7 99.5 %shard_map.114 = (bf16[4,18,16,256]{3,2,1,0:T(8,128)(2,1)S(1)}, bf16[4,32,256]{2,1,0:T(8,128)(2,1)S(1)}, bf16[4,32,256]{2,1,0:T(8,128)(2,1)S(1)}, bf16[16,432,256]{2,1,0:T(8,128)(2,1)S(1)}, f32[2,256,256]{2,1,0:T(8,128)S(1)}) custom-call(bf16[2,16,16,256]{3,2,1,0:T(8,128)(2,1)S(1)} %copy-done.2, bf16[432,256]{1,0:T(8,128)(2,1)S(1)} %copy-done.3, ...), custom_call_target="tpu_custom_call" | custom-call | tf_op jit(solution)/shard_map/pallas_call | solution.py:638
  109.2 0.0 copy-start.1
  109.2 1.0 copy-done.1
  110.2 0.0 copy-start.4
  110.2 0.8 copy-done.4
  111.0 4.7 %shard_map.115 = (bf16[128,256]{1,0:T(8,128)(2,1)}, bf16[512,256]{1,0:T(8,128)(2,1)S(1)}, f32[512,256]{1,0:T(8,128)S(1)}) custom-call(bf16[4,18,16,256]{3,2,1,0:T(8,128)(2,1)S(1)} %get-tuple-element.17.ext, bf16[4,32,256]{2,1,0:T(8,128)(2,1)S(1)} %get-tuple-element.18.left, bf16[4,32,256]{2,1,0:T(8,128)(2,1)S(1)} %get-tuple-element.19.right, ...), custom_call_target="tpu_custom_call" | custom-call | tf_op jit(solution)/shard_map/pallas_call | solution.py:666
  115.7 44.9 %shard_map.116 = (bf16[4,18,16,256]{3,2,1,0:T(8,128)(2,1)S(1)}, bf16[4,32,256]{2,1,0:T(8,128)(2,1)S(1)}, bf16[4,32,256]{2,1,0:T(8,128)(2,1)S(1)}) custom-call(bf16[2,16,16,256]{3,2,1,0:T(8,128)(2,1)S(1)} %bitcast.14), custom_call_target="tpu_custom_call" | custom-call | tf_op jit(solution)/shard_map/pallas_call | solution.py:681
  160.6 3.6 %shard_map.117 = bf16[512,256]{1,0:T(8,128)(2,1)} custom-call(bf16[4,18,16,256]{3,2,1,0:T(8,128)(2,1)S(1)} %get-tuple-element.23.ext, bf16[4,32,256]{2,1,0:T(8,128)(2,1)S(1)} %get-tuple-element.24.left, bf16[4,32,256]{2,1,0:T(8,128)(2,1)S(1)} %get-tuple-element.25.right, bf16[27,256,256]{2,1,0:T(8,128)(2,1)S(1)} %bitcast.11, ...), custom_call_target="tpu_custom_call" | custom-call | tf_op jit(solution)/shard_map/pallas_call | solution.py:691
Async XLA Ops:
  4.8 1.6 copy-start
  6.4 0.9 copy-start.2
  7.3 0.9 copy-start.3
  8.2 0.8 copy-start.5
  9.0 0.7 copy-start.6
  109.2 1.0 copy-start.1
  110.2 0.8 copy-start.4

commit v3 on v0

v3 whole, which is shorter than its diff:
```python
import jax
import jax.numpy as jnp
from jax import lax
from jax.experimental import pallas as pl
from jax.experimental.pallas import tpu as pltpu
from jax.sharding import PartitionSpec as P

MESH = pl.DeviceIdType.MESH
CAP = 2


def place():
    slab, x, strip = lax.axis_index("ta"), lax.axis_index("ha"), lax.axis_index("wa")
    return slab // 2, (slab % 2) * 8 + strip // 2, x, strip % 2


def at(y, z, x, core):
    y, z, x = (y + 4) % 4, (z + 16) % 16, (x + 4) % 4
    return (y * 2 + z // 8, x, (z % 8) * 2 + core)


class Copies:
    def __init__(self, send_sems, recv_sems):
        self.send_sems, self.recv_sems, self.used, self.sent = send_sems, recv_sems, 0, []

    def make(self, src, dst, device):
        slot = self.used
        self.used += 1
        return pltpu.make_async_remote_copy(
            src_ref=src,
            dst_ref=dst,
            send_sem=self.send_sems.at[slot],
            recv_sem=self.recv_sems.at[slot],
            device_id=device,
            device_id_type=MESH,
        )

    def start(self, src, dst, device):
        copy = self.make(src, dst, device)
        copy.start()
        self.sent.append(copy)
        return copy


def greet(devices):
    barrier = pltpu.get_barrier_semaphore()
    for device in devices:
        pl.semaphore_signal(barrier, inc=1, device_id=device, device_id_type=MESH)
    return lambda: pl.semaphore_wait(barrier, len(devices))


def edge_columns(ext, edge, frame):
    rows, cols, width = ext.shape[1:]
    flat = ext[frame].reshape(rows * cols, width)
    row = lax.broadcasted_iota(jnp.int32, (edge.shape[2], rows * cols), 0)
    cell = lax.broadcasted_iota(jnp.int32, (edge.shape[2], rows * cols), 1)
    for side, col in ((0, 0), (1, cols - 1)):
        pick = jnp.where(cell == row * cols + col, 1.0, 0.0).astype(jnp.bfloat16)
        edge[side, frame] = jnp.dot(pick, flat, preferred_element_type=jnp.float32).astype(
            jnp.bfloat16
        )


FAR = ((0, 1), (15, 1), (1, 5), (6, 5), (11, 4))


class Halo:
    def __init__(self, copies, tile, ext, left, right, edge, own, step):
        self.copies, self.tile, self.ext, self.left, self.right = copies, tile, ext, left, right
        self.edge, self.own, self.other, self.step = edge, own, 2 - own, step
        self.far = []

    def send_far(self, piece):
        y, z, x, core = place()
        y_to = y + z // 8 if self.step == 1 else y - 1 + z // 8
        first, count = FAR[piece]
        for frame in range(2):
            self.far.append(
                self.copies.start(
                    self.tile.at[frame, pl.ds(first, count)],
                    self.ext.at[self.other + frame, pl.ds(1 + first, count)],
                    at(y_to, z + 8, x, core),
                )
            )

    def own_rows(self):
        y, z, x, core = place()
        ext, own = self.ext, self.own
        self.rows_own = [
            self.copies.start(
                self.tile.at[:, pl.ds(15, 1)],
                ext.at[pl.ds(own, 2), pl.ds(0, 1)],
                at(y, z, x + 1, core),
            ),
            self.copies.start(
                self.tile.at[:, pl.ds(0, 1)],
                ext.at[pl.ds(own, 2), pl.ds(17, 1)],
                at(y, z, x - 1, core),
            ),
        ]

    def sides(self, first):
        y, z, x, core = place()
        two = pl.ds(first, 2)
        return [
            self.copies.start(
                self.edge.at[1, two], self.left.at[two], at(y, z + core, x, 1 - core)
            ),
            self.copies.start(
                self.edge.at[0, two], self.right.at[two], at(y, z - 1 + core, x, 1 - core)
            ),
        ]

    def near_columns(self):
        for copy in self.rows_own:
            copy.wait_recv()
        for frame in range(2):
            edge_columns(self.ext, self.edge, self.own + frame)
        self.near_sides = self.sides(self.own)

    def far_rows(self):
        y, z, x, core = place()
        ext, two = self.ext, pl.ds(self.other, 2)
        for copy in self.far[:4]:
            copy.wait_recv()
        self.borders = [
            self.copies.start(
                ext.at[two, pl.ds(16, 1)], ext.at[two, pl.ds(0, 1)], at(y, z, x + 1, core)
            ),
            self.copies.start(
                ext.at[two, pl.ds(1, 1)], ext.at[two, pl.ds(17, 1)], at(y, z, x - 1, core)
            ),
        ]

    def far_columns(self):
        for copy in self.far[4:] + self.borders:
            copy.wait_recv()
        for frame in range(2):
            edge_columns(self.ext, self.edge, self.other + frame)
        self.far_sides = self.sides(self.other)


def partners():
    y, z, x, core = place()
    return [
        at(y, z + 8, x, core),
        at(y + 1, z + 8, x, core),
        at(y - 1, z + 8, x, core),
        at(y, z, x + 1, core),
        at(y, z, x - 1, core),
        at(y, z, x + 1, 1 - core),
        at(y, z, x - 1, 1 - core),
        at(y, z, x + 2, core),
        at(y, z, x + 2, 1 - core),
        at(y, z, x, 1 - core),
        at(y, z + 1, x, core),
        at(y, z - 1, x, core),
        at(y, z - 1 + 2 * core, x, 1 - core),
        at(y + 1, z, x, core),
        at(y - 1, z, x, core),
    ]


def iota(shape, axis):
    return lax.broadcasted_iota(jnp.int32, shape, axis)


def ones_where(hit):
    return jnp.where(hit, 1.0, 0.0).astype(jnp.bfloat16)


def exact(pick, rows):
    return jnp.dot(pick, rows, preferred_element_type=jnp.float32)


def lay_out(index, source, cells):
    owner, frame, row, col, valid = [index[pl.ds(i, 1), pl.ds(0, 64)] for i in range(5)]
    one, other = iota((64, 64), 0), iota((64, 64), 1)

    def column(line):
        return jnp.sum(jnp.where(one == other, line, 0), 1, keepdims=True)

    before = (column(owner) == owner) & (one < other) & (column(valid) != 0)
    rank = jnp.sum(jnp.where(before, 1, 0), 0, keepdims=True)
    deep = (owner & 15) >> 1
    spot = jnp.where(deep < 4, 2 * deep + 1, 2 * (7 - deep))
    slot = (((owner >> 4) * 2 + (owner & 1)) * 8 + spot) * 2 + rank
    slot = jnp.where(valid != 0, slot, 999)
    hit = column(slot) == iota((64, 128), 1)
    source[...] = 64 + jnp.sum(jnp.where(hit, iota((64, 128), 0) - 64, 0), 0, keepdims=True)
    base = frame * 256 + row * 16 + col
    bases = [
        jnp.sum(jnp.where(slot == one * 2 + i, base, 0), 1, keepdims=True) for i in range(2)
    ]
    where = iota((64, 128), 1)
    offset = (where & 63) // 8 * 16 + (where & 7)
    cells[...] = (offset + jnp.where(where < 64, bases[0], bases[1])).reshape(8, 8, 128)


def widen(halo, wide, frames, far_there):
    _, _, x, _ = place()
    strip = lax.axis_index("wa")
    cell, other = iota((288, 288), 0), iota((288, 288), 1)
    back = ones_where((other == cell - 1) & (cell % 16 != 0))
    ahead = ones_where((other == cell + 1) & (cell % 16 != 15))
    cell, other = iota((288, 32), 0), iota((288, 32), 1)
    from_left = ones_where(cell == other * 16 + jnp.where(strip > 0, 0, 4096))
    from_right = ones_where(cell == other * 16 + 15 + jnp.where(strip < 15, 0, 4096))
    row = iota((288, 256), 0) // 16
    low, high = jnp.where(x > 0, 0, 1), jnp.where(x < 3, 17, 16)
    for frame in frames:
        far = halo.other <= frame < halo.other + 2
        least = jnp.where(far_there, low, 99) if far else low
        there = (row >= least) & (row <= high)
        flat = halo.ext[frame].reshape(288, 256)
        parts = (
            exact(back, flat) + exact(from_left, halo.left[frame]),
            flat.astype(jnp.float32),
            exact(ahead, flat) + exact(from_right, halo.right[frame]),
        )
        for shift, value in enumerate(parts):
            wide[frame, :, :, 256 * shift : 256 * shift + 256] = (
                jnp.where(there, value, 0.0).astype(jnp.bfloat16).reshape(18, 16, 256)
            )


NT = (((1,), (1,)), ((), ()))


def conv_part(wide, taps, acc, a, first, count, out):
    summed = jnp.zeros((count * 256, 256), jnp.float32)
    for b in range(3):
        at_row = (a * 3 + b) * 768
        summed += jnp.dot(
            wide[first : first + count, b : b + 16].reshape(count * 256, 768),
            taps[at_row : at_row + 768],
            preferred_element_type=jnp.float32,
        )
    acc[out * 256 : (out + count) * 256] += summed


def back_part(wide, taps, acc, a, first, count, out):
    summed = jnp.zeros((count * 256, 256), jnp.float32)
    for b in range(3):
        for c in range(3):
            at_row = ((a * 3 + b) * 3 + c) * 256
            lanes = slice(256 * (2 - c), 256 * (3 - c))
            summed += lax.dot_general(
                wide[first : first + count, 2 - b : 18 - b, :, lanes].reshape(count * 256, 256),
                taps[at_row : at_row + 256],
                NT,
                preferred_element_type=jnp.float32,
            )
    acc[out * 256 : (out + count) * 256] += summed


def middle(preact, tile, down, reduced, grad_pre, acc):
    sig = jax.nn.sigmoid(preact)
    section = (tile[...].reshape(512, 256).astype(jnp.float32) + preact * sig).astype(jnp.bfloat16)
    small, large = iota((128, 512), 0), iota((128, 512), 1)
    first = small // 64 * 256 + small // 8 % 8 * 32 + small % 8 * 2
    pooled = [
        exact(ones_where(large == first + p * 16 + q), section).astype(jnp.bfloat16)
        for p in range(2)
        for q in range(2)
    ]
    reduced[...] = jnp.dot(
        jnp.concatenate(pooled, 1), down[...].reshape(1024, 256), preferred_element_type=jnp.float32
    ).astype(jnp.bfloat16)
    spread = acc[...]
    grad_pre[...] = (spread * sig * (1.0 + preact * (1.0 - sig))).astype(jnp.bfloat16).reshape(
        2, 16, 16, 256
    )


def spread_out(down, grad_out, acc):
    large, small = iota((512, 128), 0), iota((512, 128), 1)
    over = ones_where(small == large // 256 * 64 + large // 32 % 8 * 8 + large // 2 % 8)
    repeated = exact(over, grad_out[...]).astype(jnp.bfloat16)
    cell = iota((512, 256), 0)
    kind = cell // 16 % 2 * 2 + cell % 2
    back = jnp.zeros((512, 256), jnp.float32)
    for which in range(4):
        back = jnp.where(
            kind == which,
            lax.dot_general(repeated, down[which], NT, preferred_element_type=jnp.float32),
            back,
        )
    acc[...] = back


def step_kernel(
    features, weight, indices, crop_grad, down_all, grad_all, reduced, grad_in,
    tile, index, down, grad_out, table, source, cells,
    ext, left, right, edge, ext_b, left_b, right_b, edge_b, grad_pre,
    wide, taps, preact, acc, crop, packed, crops, places, part,
    in_up, in_down, out_up, out_down,
    send_sems, recv_sems, local_sems, up_send, up_recv, down_send, down_recv,
):
    y, z, x, core = place()
    strip = z % 8
    mine = x * 2 + core
    slab = lax.axis_index("ta")
    copies = Copies(send_sems, recv_sems)

    def lane(offset):
        return pl.ds(pl.multiple_of((((strip + offset + 8) % 8) * 2 + core) * 432, 16), 432)

    loads = [
        pltpu.make_async_copy(src, dst, local_sems.at[i])
        for i, (src, dst) in enumerate(
            (
                (indices, index),
                (crop_grad, crop.at[pl.ds(0, 64)]),
                (features, tile),
                (weight, taps.at[lane(0)]),
                (down_all, down),
                (grad_all, grad_out),
            )
        )
    ]
    for load in loads:
        load.start()
    met = greet(partners())
    crop[64] = jnp.zeros_like(crop[64])
    loads[0].wait()
    lay_out(index, table, cells)
    to_scalars = pltpu.make_async_copy(table, source, local_sems.at[6])
    to_scalars.start()
    places[mine] = cells[mine]
    loads[2].wait()
    ext[2:4, 1:17] = tile[...]
    loads[1].wait()
    to_scalars.wait()

    near = [
        (away, flip, ((x + away + 4) % 4) * 2 + (core + flip) % 2)
        for away in (2, 1, -1)
        for flip in range(2)
    ] + [(0, 1, x * 2 + 1 - core)]

    def pack(dest):
        def fill(i, _):
            packed[dest, i // 4, i // 2 % 2, pl.ds(i % 2 * 64, 64)] = crop[source[0, dest * 16 + i]]
            return 0

        lax.fori_loop(0, 16, fill, 0)

    for _, _, dest in near:
        pack(dest)

    def keep(i, _):
        crops[i // 4, i // 2 % 2, mine, pl.ds(i % 2 * 64, 64)] = crop[source[0, mine * 16 + i]]
        return 0

    lax.fori_loop(0, 16, keep, 0)
    for load in loads[3:]:
        load.wait()
    halo = Halo(copies, tile, ext, left, right, edge, 2, 1)
    back = Halo(copies, grad_pre, ext_b, left_b, right_b, edge_b, 0, -1)
    half = pl.ds(pl.multiple_of((y % 2) * 128, 128), 128)
    turn = 1 - 2 * core

    def crops_send(group):
        return [
            copies.start(
                packed.at[dest, group],
                crops.at[group, :, mine],
                at(y, z, x + away, (core + flip) % 2),
            )
            for away, flip, dest in near
        ]

    met()
    arriving, ring, swaps = {}, {}, {}
    halo.send_far(0)
    halo.send_far(1)
    for way in (1, -1):
        piece = taps.at[lane(0), half]
        ring[way] = copies.start(piece, piece, at(y, z + way, x, core))
    halo.own_rows()
    marks = [
        copies.start(cells.at[dest], places.at[mine], at(y, z, x + away, (core + flip) % 2))
        for away, flip, dest in near
    ]
    arriving[0] = crops_send(0)
    halo.send_far(2)
    rest = [copies.start(taps.at[lane(0)], taps.at[lane(0)], at(y, z, x, 1 - core))]

    def swap(offset, y_to):
        piece = taps.at[lane(offset), half]
        swaps[offset] = copies.start(piece, piece, at(y_to, z, x, core))

    def ring_step(step):
        for way in (1, -1):
            ring[way].wait_recv()
            offset = -way * step
            if step < 3:
                piece = taps.at[lane(offset), half]
                ring[way] = copies.start(piece, piece, at(y, z + way, x, core))
            swap(offset, y + way)

    def whole(offset):
        swaps[offset].wait_recv()
        shard_all = taps.at[lane(offset)]
        rest.append(copies.start(shard_all, shard_all, at(y, z, x, 1 - core)))

    cell = iota((512, 128), 0)

    def settle(group):
        for copy in arriving[group] + (marks if group == 0 else []):
            copy.wait_recv()
        for i in range(2):
            goal = 7 - group if i == 0 else group
            part[goal] = jnp.zeros_like(part[goal])

            def add(pair, _):
                hits = [
                    ones_where(cell == places[2 * pair + j, 2 * group + i][None, :])
                    for j in range(2)
                ]
                part[goal] += jnp.dot(
                    jnp.concatenate(hits, 1),
                    crops[group, i, pl.ds(2 * pair, 2)].reshape(256, 256),
                    preferred_element_type=jnp.float32,
                )
                return 0

            lax.fori_loop(0, 4, add, 0)

    def chain(goal, chunk, way):
        landing, leaving, sends, recvs = (
            (in_up, out_up, up_send, up_recv) if way == 1 else (in_down, out_down, down_send, down_recv)
        )
        return pltpu.make_async_remote_copy(
            src_ref=leaving.at[goal, chunk],
            dst_ref=landing.at[goal, chunk],
            send_sem=sends.at[goal, chunk],
            recv_sem=recvs.at[goal, chunk],
            device_id=at(y, z + way, x, core),
            device_id_type=MESH,
        )

    def turn_of(step, way):
        rank = strip if way == 1 else 7 - strip
        turn_at = step - rank + 16
        late = (turn_at - 16 + 32) % 32
        odd = late % 2
        ahead = (1 - odd) * (7 - late // 2) + odd * (late // 2)
        busy = (late < 8) & (late != 1) & (rank < ahead)
        return rank, (ahead if way == 1 else 7 - ahead), busy

    def advance(step, chunk, way):
        rank, goal, busy = turn_of(step, way)
        landing, leaving = (in_up, out_up) if way == 1 else (in_down, out_down)

        @pl.when(busy)
        def _():
            copy = chain(goal, chunk, way)
            mid = part[goal, pl.ds(chunk * 256, 256)]

            @pl.when(rank > 0)
            def _():
                copy.wait_recv()
                leaving[goal, chunk] = (mid + landing[goal, chunk].astype(jnp.float32)).astype(
                    jnp.bfloat16
                )

            @pl.when(rank == 0)
            def _():
                leaving[goal, chunk] = mid.astype(jnp.bfloat16)

            copy.start()

    def slot(step):
        for chunk in range(2):
            for way in (1, -1):
                advance(step, chunk, way)

    ring_step(1)
    halo.send_far(3)
    halo.far_rows()
    arriving[1] = crops_send(1)
    halo.near_columns()
    ring_step(2)
    halo.send_far(4)
    spread_out(down, grad_out, acc)
    settle(0)
    slot(0)
    arriving[2] = crops_send(2)
    ring_step(3)
    piece = taps.at[lane(-3 * turn), half]
    ring_last = copies.start(piece, piece, at(y, z + turn, x, core))
    for offset in (1, -1, 2, -2):
        whole(offset)
    slot(1)
    ring_last.wait_recv()
    swap(4, y + turn)
    settle(1)
    slot(2)
    arriving[3] = crops_send(3)
    for offset in (3, -3, 4):
        whole(offset)
    for copy in halo.near_sides + rest:
        copy.wait_recv()
    preact[...] = jnp.zeros_like(preact)
    widen(halo, wide, (2, 3), slab > 0)
    conv_part(wide, taps, preact, 2, 2, 2, 0)
    slot(3)
    conv_part(wide, taps, preact, 1, 2, 1, 1)
    halo.far_columns()
    settle(2)
    slot(4)
    for copy in halo.far_sides:
        copy.wait_recv()
    widen(halo, wide, (0, 1), slab > 0)
    conv_part(wide, taps, preact, 0, 0, 2, 0)
    conv_part(wide, taps, preact, 1, 1, 1, 0)
    middle(preact[...], tile, down, reduced, grad_pre, acc)
    back.send_far(0)
    back.send_far(1)
    back.own_rows()
    back.send_far(2)
    ext_b[0:2, 1:17] = grad_pre[...]
    slot(5)
    back.send_far(3)
    settle(3)
    slot(6)
    back.near_columns()
    back.send_far(4)
    slot(7)
    back.far_rows()
    slot(8)
    for copy in back.near_sides:
        copy.wait_recv()
    widen(back, wide, (0, 1), slab < 7)
    slot(9)
    back_part(wide, taps, acc, 2, 0, 2, 0)
    back_part(wide, taps, acc, 1, 1, 1, 0)
    back.far_columns()
    assert copies.used == SENDS, copies.used
    for chunk in range(2):
        place_at = pl.ds(chunk * 256, 256)
        acc[place_at] += part[strip, place_at]
        for way in (1, -1):
            landing = in_up if way == 1 else in_down

            @pl.when((strip if way == 1 else 7 - strip) > 0)
            def _():
                chain(strip, chunk, way).wait_recv()
                acc[place_at] += landing[strip, chunk].astype(jnp.float32)

    for copy in back.far_sides:
        copy.wait_recv()
    widen(back, wide, (2, 3), slab < 7)
    back_part(wide, taps, acc, 0, 2, 2, 0)
    back_part(wide, taps, acc, 1, 2, 1, 1)
    grad_in[...] = acc[...].astype(jnp.bfloat16)
    for step in range(10):
        for chunk in range(2):
            for way in (1, -1):
                rank, goal, busy = turn_of(step, way)

                @pl.when(busy)
                def _():
                    chain(goal, chunk, way).wait_send()

    for copy in copies.sent:
        copy.wait_send()


SENDS = 93
DMA = pltpu.SemaphoreType.DMA


def per_device(
    features, conv_weight, down_weight, grad_out, crop_grad,
    crop_owner, crop_frame, crop_row, crop_col, crop_valid,
):
    frames, rows, cols, width = features.shape
    half_type, shape, vmem = jnp.bfloat16, jax.ShapeDtypeStruct, pltpu.VMEM
    indices = jnp.stack(
        [crop_owner[:, 0], crop_frame, crop_row, crop_col, crop_valid] + [crop_valid] * 3, 0
    )
    indices = jnp.pad(indices, ((0, 0), (0, 64)))
    halo = [
        vmem((4, 18, 16, width), half_type), vmem((4, 32, width), half_type),
        vmem((4, 32, width), half_type), vmem((2, 4, 32, width), half_type),
    ]
    tile = vmem((2, 16, 16, width), half_type)
    chain = vmem((8, 2, 256, width), half_type)
    reduced, grad_in = pl.pallas_call(
        step_kernel,
        out_shape=(shape((128, width), half_type), shape((512, width), half_type)),
        in_specs=[pl.BlockSpec(memory_space=pl.ANY)] * 6,
        out_specs=[pl.BlockSpec(memory_space=pltpu.VMEM)] * 2,
        scratch_shapes=[
            tile, vmem((8, 128), jnp.int32), vmem((4, width, width), half_type),
            vmem((128, width), half_type), vmem((1, 128), jnp.int32),
            pltpu.SMEM((1, 128), jnp.int32), vmem((8, 8, 128), jnp.int32),
            *halo, *halo, tile,
            vmem((4, 18, 16, 3 * width), half_type), vmem((6912, width), half_type),
            vmem((512, width), jnp.float32), vmem((512, width), jnp.float32),
            vmem((65, 64, width), half_type), vmem((8, 4, 2, 128, width), half_type),
            vmem((4, 2, 8, 128, width), half_type), vmem((8, 8, 128), jnp.int32),
            vmem((8, 512, width), jnp.float32),
            chain, chain, chain, chain,
            DMA((SENDS,)), DMA((SENDS,)), DMA((7,)),
            DMA((8, 2)), DMA((8, 2)), DMA((8, 2)), DMA((8, 2)),
        ],
        compiler_params=pltpu.CompilerParams(
            collective_id=0, has_side_effects=True, vmem_limit_bytes=60 << 20
        ),
    )(
        features, conv_weight, indices, crop_grad.reshape(64, 64, width),
        down_weight.reshape(4, width, width), grad_out.reshape(-1, width),
    )
    return (
        reduced.reshape(frames, rows // 2, cols // 2, width),
        grad_in.reshape(frames, rows, cols, width),
    )


def solution(mesh):
    spread_all = ("ta", "ha", "wa")
    tile = P("ta", "ha", "wa", None)
    in_specs = (
        tile, P("wa", None), P(), tile, P(spread_all, None, None, None), P(spread_all, None),
        P(spread_all), P(spread_all), P(spread_all), P(spread_all),
    )
    return jax.shard_map(
        per_device, mesh=mesh, in_specs=in_specs, out_specs=(tile, tile), check_vma=False
    )
```

time: 449 us -> 131 us (0.29)
  the two profiles are of different devices: /device:TPU:29 before, /device:TPU:35 now
where the time goes in v3:
time: 131 us
  Pallas kernels  126 us (96%)
  local copies, waits for them, and re-layouts  4.56 us (3%)
    pallas_call x1, Pallas kernels, per_device(): pl.pallas_call(step_kernel, out_shape=(shape((128, width), half_type), sh...  126 us
    unnamed x2, local copies, waits for them, and re-layouts  3.14 us

profile of v3, /device:TPU:35, one launch (start us, length us, event | category | flops | bytes accessed | tf_op | source)
XLA Modules:
  0.0 131.3 jit_solution(12602553209575265480)
XLA Ops:
  0.6 0.8 stack.22
  1.5 0.6 pad.4.indices
  2.1 126.0 %shard_map.113 = (bf16[128,256]{1,0:T(8,128)(2,1)}, bf16[512,256]{1,0:T(8,128)(2,1)}) custom-call(bf16[2,16,16,256]{3,2,1,0:T(8,128)(2,1)} %features.1, bf16[432,256]{1,0:T(8,128)(2,1)} %weight.1, s32[8,128]{1,0:T(8,128)} %pad.4.indices, bf16[64,64,256]{2,1,0:T(8,128)(2,1)} %bitcast.10, bf16[4,256,256]{2,1,0:T(8,128)(2,1)} %bitcast.11, bf16[128,256]{1,0:T(8,128)(2,1)} %bitcast.13), custom_call_target="tpu_custom_call" | custom-call | tf_op jit(solution)/shard_map/pallas_call | solution.py:592
  128.1 1.5 %copy.14 = bf16[2,8,8,256]{3,2,1,0:T(8,128)(2,1)} copy(bf16[2,8,8,256]{3,2,1,0:T(8,128)(2,1)} %bitcast.14) | data formatting | bytes 131072
  129.6 1.7 %copy.15 = bf16[2,16,16,256]{3,2,1,0:T(8,128)(2,1)} copy(bf16[2,16,16,256]{3,2,1,0:T(8,128)(2,1)} %bitcast.12) | data formatting | bytes 524288

commit v4 on v3

--- a/solution.py
+++ b/solution.py
@@ -174,7 +174,7 @@
 
 
 def lay_out(index, source, cells):
-    owner, frame, row, col, valid = [index[pl.ds(i, 1), pl.ds(0, 64)] for i in range(5)]
+    owner, frame, row, col, valid = [index[pl.ds(i, 1), :] for i in range(5)]
     one, other = iota((64, 64), 0), iota((64, 64), 1)
 
     def column(line):
@@ -569,6 +569,11 @@
         copy.wait_send()
 
 
+def hand_on(reduced, grad_in, reduced_out, grad_out):
+    reduced_out[...] = reduced[...]
+    grad_out[...] = grad_in[...]
+
+
 SENDS = 93
 DMA = pltpu.SemaphoreType.DMA
 
@@ -582,7 +587,6 @@
     indices = jnp.stack(
         [crop_owner[:, 0], crop_frame, crop_row, crop_col, crop_valid] + [crop_valid] * 3, 0
     )
-    indices = jnp.pad(indices, ((0, 0), (0, 64)))
     halo = [
         vmem((4, 18, 16, width), half_type), vmem((4, 32, width), half_type),
         vmem((4, 32, width), half_type), vmem((2, 4, 32, width), half_type),
@@ -595,7 +599,7 @@
         in_specs=[pl.BlockSpec(memory_space=pl.ANY)] * 6,
         out_specs=[pl.BlockSpec(memory_space=pltpu.VMEM)] * 2,
         scratch_shapes=[
-            tile, vmem((8, 128), jnp.int32), vmem((4, width, width), half_type),
+            tile, vmem((8, 64), jnp.int32), vmem((4, width, width), half_type),
             vmem((128, width), half_type), vmem((1, 128), jnp.int32),
             pltpu.SMEM((1, 128), jnp.int32), vmem((8, 8, 128), jnp.int32),
             *halo, *halo, tile,
@@ -615,6 +619,12 @@
         features, conv_weight, indices, crop_grad.reshape(64, 64, width),
         down_weight.reshape(4, width, width), grad_out.reshape(-1, width),
     )
+    reduced, grad_in = pl.pallas_call(
+        hand_on,
+        out_shape=(shape((128, width), half_type), shape((512, width), half_type)),
+        in_specs=[pl.BlockSpec(memory_space=pltpu.VMEM)] * 2,
+        out_specs=[pl.BlockSpec(memory_space=pltpu.VMEM)] * 2,
+    )(reduced, grad_in)
     return (
         reduced.reshape(frames, rows // 2, cols // 2, width),
         grad_in.reshape(frames, rows, cols, width),

time: 131 us -> 130 us (level)
  the two profiles are of different devices: /device:TPU:35 before, /device:TPU:1 now
where the time goes in v4:
time: 130 us; the launch traced here: 127 us
  Pallas kernels  125 us (96%)
  local copies, waits for them, and re-layouts  1.41 us (1%)
    pallas_call x1, Pallas kernels, per_device(): pl.pallas_call(step_kernel, out_shape=(shape((128, width), half_type), sh...  124 us

profile of v4, /device:TPU:1, one launch (start us, length us, event | category | flops | bytes accessed | tf_op | source)
XLA Modules:
  0.0 127.4 jit_solution(15107588995247061348)
XLA Ops:
  0.6 1.4 %stack.22.indices = s32[8,64]{1,0:T(8,128)} concatenate(s32[1,64]{1,0:T(1,128)} %bitcast.17, s32[1,64]{1,0:T(1,128)} %bitcast.18, s32[1,64]{1,0:T(1,128)} %bitcast.19, s32[1,64]{1,0:T(1,128)} %bitcast.20, s32[1,64]{1,0:T(1,128)} %bitcast.13, s32[1,64]{1,0:T(1,128)} %bitcast.14, s32[1,64]{1,0:T(1,128)} %bitcast.15, s32[1,64]{1,0:T(1,128)} %bitcast.16), dimensions={0} | concatenate | bytes 4096 | tf_op jit(solution)/shard_map/stack | solution.py:587
  2.0 123.6 %shard_map.113 = (bf16[128,256]{1,0:T(8,128)(2,1)}, bf16[512,256]{1,0:T(8,128)(2,1)}) custom-call(bf16[2,16,16,256]{3,2,1,0:T(8,128)(2,1)} %features.1, bf16[432,256]{1,0:T(8,128)(2,1)} %weight.1, s32[8,64]{1,0:T(8,128)} %stack.22.indices, bf16[64,64,256]{2,1,0:T(8,128)(2,1)} %bitcast.10, bf16[4,256,256]{2,1,0:T(8,128)(2,1)} %bitcast.11, ...), custom_call_target="tpu_custom_call" | custom-call | tf_op jit(solution)/shard_map/pallas_call | solution.py:596
  125.7 1.7 %shard_map.114 = (bf16[128,256]{1,0:T(8,128)(2,1)}, bf16[512,256]{1,0:T(8,128)(2,1)}) custom-call(bf16[128,256]{1,0:T(8,128)(2,1)} %get-tuple-element.6.reduced, bf16[512,256]{1,0:T(8,128)(2,1)} %get-tuple-element.7.grad_in), custom_call_target="tpu_custom_call" | custom-call | tf_op jit(solution)/shard_map/pallas_call | solution.py:622

commit v5 on v4

--- a/solution.py
+++ b/solution.py
@@ -521,13 +521,13 @@
     back.send_far(1)
     back.own_rows()
     back.send_far(2)
+    back.send_far(3)
     ext_b[0:2, 1:17] = grad_pre[...]
     slot(5)
-    back.send_far(3)
+    back.send_far(4)
     settle(3)
     slot(6)
     back.near_columns()
-    back.send_far(4)
     slot(7)
     back.far_rows()
     slot(8)

time: 130 us -> 130 us (level)
  no operation moved by 1% of the time
where the time goes in v5:
time: 130 us; the launch traced here: 127 us
  Pallas kernels  125 us (96%)
  local copies, waits for them, and re-layouts  1.41 us (1%)
    pallas_call x1, Pallas kernels, per_device(): pl.pallas_call(step_kernel, out_shape=(shape((128, width), half_type), sh...  124 us

profile of v5, /device:TPU:1, one launch (start us, length us, event | category | flops | bytes accessed | tf_op | source)
XLA Modules:
  0.0 127.4 jit_solution(11004948871323858842)
XLA Ops:
  0.6 1.4 %stack.22.indices = s32[8,64]{1,0:T(8,128)} concatenate(s32[1,64]{1,0:T(1,128)} %bitcast.17, s32[1,64]{1,0:T(1,128)} %bitcast.18, s32[1,64]{1,0:T(1,128)} %bitcast.19, s32[1,64]{1,0:T(1,128)} %bitcast.20, s32[1,64]{1,0:T(1,128)} %bitcast.13, s32[1,64]{1,0:T(1,128)} %bitcast.14, s32[1,64]{1,0:T(1,128)} %bitcast.15, s32[1,64]{1,0:T(1,128)} %bitcast.16), dimensions={0} | concatenate | bytes 4096 | tf_op jit(solution)/shard_map/stack | solution.py:587
  2.0 123.6 %shard_map.113 = (bf16[128,256]{1,0:T(8,128)(2,1)}, bf16[512,256]{1,0:T(8,128)(2,1)}) custom-call(bf16[2,16,16,256]{3,2,1,0:T(8,128)(2,1)} %features.1, bf16[432,256]{1,0:T(8,128)(2,1)} %weight.1, s32[8,64]{1,0:T(8,128)} %stack.22.indices, bf16[64,64,256]{2,1,0:T(8,128)(2,1)} %bitcast.10, bf16[4,256,256]{2,1,0:T(8,128)(2,1)} %bitcast.11, ...), custom_call_target="tpu_custom_call" | custom-call | tf_op jit(solution)/shard_map/pallas_call | solution.py:596
  125.7 1.7 %shard_map.114 = (bf16[128,256]{1,0:T(8,128)(2,1)}, bf16[512,256]{1,0:T(8,128)(2,1)}) custom-call(bf16[128,256]{1,0:T(8,128)(2,1)} %get-tuple-element.6.reduced, bf16[512,256]{1,0:T(8,128)(2,1)} %get-tuple-element.7.grad_in), custom_call_target="tpu_custom_call" | custom-call | tf_op jit(solution)/shard_map/pallas_call | solution.py:622
